TPU v7x, 512 devices: a whole 4x8x8 slice. The times are simulated.
512 devices in a mesh: grp: 16 (over x, z_hi, core), dev: 32 (over y, z_lo).
Axes of the slice: x: 4, y: 8, z: 8 (z_hi: 2, z_lo: 4; z = z_hi * 4 + z_lo), core: 2. Of those that a mesh axis runs over, the one named last changes fastest.
Arguments:
- adjoint: bfloat16 [1024, 30, 192], P(('grp', 'dev')), may hold values from -6 to 6
- jacobian_tiles: bfloat16 [1024, 17, 36864], P(('grp', 'dev'))
- columns: int32 [1024, 16], P(('grp', 'dev')), may hold values from 0 to 127, as said below
- cell_rates: float32 [1024, 192], P(('grp', 'dev')), may hold values from 0.05 to 0.5
- precond: bfloat16 [1024, 36864], P(('grp', 'dev')), may hold values from -0.4375 to 0.4375
- lower_list: int32 [16, 32], replicated, may hold values from 0 to 63, as said below
- upper_list: int32 [16, 32], replicated, may hold values from 0 to 63, as said below
Outputs:
- preconditioned: bfloat16 [1024, 30, 192], P(('grp', 'dev'))
Inputs may be any that keep to these rules, and one draw needn't show every extreme that they name: `columns`: rows of the first group name no value in 64 .. 95, rows of the last group no value of 96 or more. `lower_list`: the entries of a row are distinct. `upper_list`: the entries of a row are distinct.
All inputs are finite; a program needn't handle non-finite values.
Results may differ from a plain program's by a relative error of at most 0.005.
Values sent between devices are 32-bit elements; how exact they have to be, the bound alone decides.
No kernel may reach another device: no remote copies, remote signals or barrier semaphores. Data moves between devices by JAX's collectives and lax.ppermute only.
A program may use at most 64 MiB of HBM per device.

v0:
```python
import jax
import jax.numpy as jnp
from jax import lax
from jax.experimental import pallas as pl
from jax.experimental.pallas import tpu as pltpu
from jax.sharding import Mesh, PartitionSpec as P

INST = 15
ADJ = 2
HALO = 32
GROUP_BLOCKS = 64
AXES = ("x", "zh", "core", "yh", "yp", "zq", "zp")
SIZES = (4, 2, 2, 4, 2, 2, 2)
PLANES = (48, 128)
KEEP, GIVE, OFF, ON, ROWS = 0, 32, 64, 96, 128


def spectral_matrix(length):
    row_index = jnp.arange(length)[:, None]
    col_index = jnp.arange(length)[None, :]
    offset = row_index - col_index
    parity = jnp.where(offset % 2 == 0, 1.0, -1.0).astype(jnp.float32)
    phase_angle = jnp.pi / length * offset.astype(jnp.float32)
    sine_values = jnp.where(offset == 0, 1.0, jnp.sin(phase_angle))
    return jnp.where(offset == 0, 0.0, 0.5 * parity / sine_values)


def mate_of(core, y):
    return ((((y - core) % 8) ^ 1) + core) % 8


def to_mate(value):
    pairs = [(c * 8 + y, c * 8 + mate_of(c, y)) for c in range(2) for y in range(8)]
    return lax.ppermute(value, ("core", "yh", "yp"), pairs)


def to_side(value):
    return lax.ppermute(value, "zp", [(0, 1), (1, 0)])


def to_mates_side(value):
    pairs = [
        (c * 16 + y * 2 + z, c * 16 + mate_of(c, y) * 2 + 1 - z)
        for c in range(2)
        for y in range(8)
        for z in range(2)
    ]
    return lax.ppermute(value, ("core", "yh", "yp", "zp"), pairs)


def off_chip_pairs():
    pairs = []
    for g in range(16):
        t = g + 1 if g % 2 else g - 1
        if 0 <= t < 16:
            pairs += [(g * 4 + z, t * 4 + 3 - z) for z in range(4)]
    return pairs


def group_index():
    return (lax.axis_index("x") * 2 + lax.axis_index("zh")) * 2 + lax.axis_index("core")


def row_of(block):
    return ((block >> 4) << 3) + (block & 7)


def parity_of(block):
    return (block >> 3) & 1


def terms_kernel(columns, lower, upper, adj, tiles, sums, own, side, mate, cross, on):
    odd, mine = lax.axis_index("core"), lax.axis_index("yp")
    quarter = mine * 2 + lax.axis_index("zp")
    off_base = GROUP_BLOCKS + HALO * odd
    on_base = GROUP_BLOCKS + HALO * (1 - odd)
    for i in range(ROWS):
        sums[i] = jnp.zeros(PLANES, jnp.float32)
    for b in range(2):
        rows = adj[b]
        for k in range(17):
            term = jnp.dot(rows, tiles[k, b], preferred_element_type=jnp.float32)
            tail = jnp.concatenate([term[:16, 128:], term[16:, 128:]], axis=1)
            planes = jnp.concatenate([term[:16, :128], term[16:, :128], tail], axis=0)
            if k == 0:
                target = lax.axis_index("yh") * 8 + lax.axis_index("zq") * 4 + lax.axis_index("zp") * 2 + b
            else:
                c = columns[b, k - 1]
                slot = c - off_base
                target = jnp.where(
                    c < GROUP_BLOCKS,
                    ((parity_of(c) ^ mine) << 5) + row_of(c),
                    jnp.where(
                        (slot >= 0) & (slot < HALO),
                        OFF + (((slot >> 3) ^ quarter) << 3) + (slot & 7),
                        ON + c - on_base,
                    ),
                )
            sums[target] += planes
    own[...] = sums[OFF : OFF + 8]
    side[...] = sums[OFF + 8 : OFF + 16]
    mate[...] = sums[OFF + 16 : OFF + 24]
    cross[...] = sums[OFF + 24 : OFF + 32]
    on[...] = sums[ON : ON + HALO]


def quarter_kernel(side, mate, cross, own, leaving):
    leaving[...] = (own[...] + side[...]) + (mate[...] + cross[...])


def merge_kernel(lower, upper, got_on, sums, keep, give):
    sibling, odd = group_index() ^ 1, lax.axis_index("core")
    mine = lax.axis_index("yp")
    keep[...] = sums[KEEP : KEEP + 32]
    give[...] = sums[GIVE : GIVE + 32]
    for h in range(HALO):
        block = jnp.where(odd == 1, upper[sibling, h], lower[sibling, h])
        same = parity_of(block) == mine
        row = row_of(block)

        @pl.when(same)
        def _():
            keep[row] += got_on[h]

        @pl.when(jnp.logical_not(same))
        def _():
            give[row] += got_on[h]


def place_kernel(lower, upper, keep, got, crossed, passed, out):
    group, odd = group_index(), lax.axis_index("core")
    mine = lax.axis_index("yp")
    above = jnp.minimum(group + 1, lower.shape[0] - 1)
    below = jnp.maximum(group - 1, 0)
    out[...] = keep[...] + got[...]
    mirrored = 1 - lax.axis_index("zp")
    for i in range(8):
        for source, parity in ((crossed, mine), (passed, 1 - mine)):
            slot = parity * 16 + mirrored * 8 + i
            block = jnp.where(odd == 1, lower[above, slot], upper[below, slot])
            row = row_of(block)

            @pl.when(parity_of(block) == mine)
            def _():
                out[row] += source[i]


def spectral_kernel(matrix, adj, rates, out):
    for b in range(2):
        part = jnp.dot(
            matrix[...],
            adj[b].astype(jnp.float32),
            precision=lax.Precision.HIGHEST,
            preferred_element_type=jnp.float32,
        )
        out[b] = rates[b : b + 1, :] * part


def last_kernel(shared, part, precond, out):
    for b in range(2):
        total = shared[0, b]
        for i in range(1, 16):
            total += shared[i, b]
        tail = total[32:48]
        top = jnp.concatenate([total[:16], tail[:, :64]], axis=1)
        bottom = jnp.concatenate([total[16:32], tail[:, 64:]], axis=1)
        combined = (jnp.concatenate([top, bottom], axis=0) + part[b]).astype(jnp.bfloat16)
        out[b] = jnp.dot(combined, precond[b], preferred_element_type=jnp.float32).astype(
            jnp.bfloat16
        )


def whole():
    return pl.BlockSpec(memory_space=pltpu.VMEM)


def scalars():
    return pl.BlockSpec(memory_space=pltpu.SMEM)


def stack(*counts):
    return [jax.ShapeDtypeStruct((n,) + PLANES, jnp.float32) for n in counts]


def shards(adjoint, jacobian_tiles, columns, cell_rates, precond, lower_list, upper_list):
    blocks, row_count, tile_width = adjoint.shape
    slots = jacobian_tiles.shape[1]
    tiles = jacobian_tiles.reshape(blocks, slots, tile_width, tile_width).transpose(1, 0, 2, 3)
    square_precond = precond.reshape(blocks, tile_width, tile_width)
    padded = jnp.pad(
        adjoint.reshape(blocks, ADJ, INST, tile_width), ((0, 0), (0, 0), (0, 1), (0, 0))
    ).reshape(blocks, 32, tile_width)

    sums, own, side, mate, cross, on = pl.pallas_call(
        terms_kernel,
        out_shape=stack(ROWS, 8, 8, 8, 8, HALO),
        in_specs=[scalars(), scalars(), scalars(), whole(), whole()],
        out_specs=[whole()] * 6,
        compiler_params=pltpu.CompilerParams(vmem_limit_bytes=32 * 2**20),
        name="terms",
    )(columns, lower_list, upper_list, padded, tiles)
    leaving = pl.pallas_call(
        quarter_kernel,
        out_shape=stack(8)[0],
        in_specs=[whole()] * 4,
        out_specs=whole(),
        compiler_params=pltpu.CompilerParams(vmem_limit_bytes=16 * 2**20),
        name="quarter",
    )(to_side(side), to_mate(mate), to_mates_side(cross), own)
    leaving, on = lax.optimization_barrier((leaving, on))
    crossed = lax.ppermute(leaving, ("x", "zh", "core", "zq", "zp"), off_chip_pairs())
    got_on = lax.ppermute(on, "core", [(0, 1), (1, 0)])
    keep, give = pl.pallas_call(
        merge_kernel,
        out_shape=stack(32, 32),
        in_specs=[scalars(), scalars()] + [whole()] * 2,
        out_specs=[whole()] * 2,
        compiler_params=pltpu.CompilerParams(vmem_limit_bytes=24 * 2**20),
        name="merge",
    )(lower_list, upper_list, got_on, sums)
    got = to_mate(give)
    passed = to_mate(crossed)
    merged = pl.pallas_call(
        place_kernel,
        out_shape=stack(32)[0],
        in_specs=[scalars(), scalars()] + [whole()] * 4,
        out_specs=whole(),
        compiler_params=pltpu.CompilerParams(vmem_limit_bytes=16 * 2**20),
        name="place",
    )(lower_list, upper_list, keep, got, crossed, passed)
    shared = lax.all_to_all(merged.reshape(16, -1), ("yh", "zq", "zp"), 0, 0, tiled=True)

    half = jnp.pad(spectral_matrix(INST).T, ((0, 1), (0, 1)))
    matrix = jnp.kron(jnp.eye(ADJ, dtype=jnp.float32), half)
    part = pl.pallas_call(
        spectral_kernel,
        out_shape=jax.ShapeDtypeStruct((blocks, 32, tile_width), jnp.float32),
        in_specs=[whole()] * 3,
        out_specs=whole(),
        compiler_params=pltpu.CompilerParams(vmem_limit_bytes=8 * 2**20),
        name="spectral",
    )(matrix, padded, cell_rates)
    result = pl.pallas_call(
        last_kernel,
        out_shape=jax.ShapeDtypeStruct((blocks, 32, tile_width), jnp.bfloat16),
        in_specs=[whole()] * 3,
        out_specs=whole(),
        compiler_params=pltpu.CompilerParams(vmem_limit_bytes=8 * 2**20),
        name="last",
    )(shared.reshape(16, blocks, *PLANES), part, square_precond)
    return (
        result.reshape(blocks, ADJ, 16, tile_width)[:, :, :INST]
        .reshape(blocks, row_count, tile_width)
    )


def solution(mesh):
    split_mesh = Mesh(mesh.devices.reshape(SIZES), AXES)
    split = P(AXES)
    return jax.shard_map(
        shards,
        mesh=split_mesh,
        in_specs=(split, split, split, split, split, P(), P()),
        out_specs=split,
        check_vma=False,
    )
```

profile of v0, /device:TPU:2, one launch (start us, length us, event | category | flops | bytes accessed | tf_op | source)
XLA Modules:
  0.0 95.9 jit_solution(17285562961363527527)
XLA Ops:
  0.0 0.8 copy.10
  0.8 6.3 %reshape.42 = bf16[2,17,192,192]{3,2,0,1:T(8,128)(2,1)S(1)} reshape(bf16[2,17,36864]{2,0,1:T(2,128)(2,1)} %param.8) | data formatting | bytes 5013504 | tf_op jit(solution)/shard_map/reshape | solution.py:188
  7.1 1.8 %terms.1 = (f32[128,48,128]{2,1,0:T(8,128)S(1)}, f32[8,48,128]{2,1,0:T(8,128)S(1)}, f32[8,48,128]{2,1,0:T(8,128)S(1)}, f32[8,48,128]{2,1,0:T(8,128)S(1)}, f32[8,...) custom-call(s32[2,16]{1,0:T(2,128)S(1)} %copy-done.3, s32[16,32]{1,0:T(8,128)S(1)} %copy-done, s32[16,32]{1,0:T(8,128)S(1)} %copy-done.1, ...), custom_call_target="tpu_custom_call" | custom-call | tf_op jit(solution)/shard_map/terms/pallas_call | solution.py:194
  8.9 4.3 %collective-permute-start = (f32[8,48,128]{2,1,0:T(8,128)S(1)}, f32[8,48,128]{2,1,0:T(8,128)S(1)}, u32[]{:S(2)}, u32[]{:S(2)}) collective-permute-start(f32[8,48,128]{2,1,0:T(8,128)S(1)} %get-tuple-element.15), channel_id=1, source_target_pairs={{0,1},{1,0},{2,3},{3,2},{4,5},{5,4},{6,7},{7,6},{8,9},{9,8},{10,11... | collective-permute-start | bytes 589832 | tf_op jit(solution)/shard_map/ppermute | solution.py:38
  13.2 3.5 %collective-permute-start.1 = (f32[8,48,128]{2,1,0:T(8,128)S(1)}, f32[8,48,128]{2,1,0:T(8,128)S(1)}, u32[]{:S(2)}, u32[]{:S(2)}) collective-permute-start(f32[8,48,128]{2,1,0:T(8,128)S(1)} %get-tuple-element.16), channel_id=1, source_target_pairs={{0,4},{4,0},{8,12},{12,8},{16,20},{20,16},{24,28},{28,24},{32,60},... | collective-permute-start | bytes 589832 | tf_op jit(solution)/shard_map/ppermute | solution.py:34
  16.7 1.9 %collective-permute-start.2 = (f32[8,48,128]{2,1,0:T(8,128)S(1)}, f32[8,48,128]{2,1,0:T(8,128)S(1)}, u32[]{:S(2)}, u32[]{:S(2)}) collective-permute-start(f32[8,48,128]{2,1,0:T(8,128)S(1)} %get-tuple-element.17), channel_id=1, source_target_pairs={{0,5},{1,4},{4,1},{5,0},{8,13},{9,12},{12,9},{13,8},{16,21},{17,20... | collective-permute-start | bytes 589832 | tf_op jit(solution)/shard_map/ppermute | solution.py:48
  18.7 2.1 %collective-permute-done.1.mate = f32[8,48,128]{2,1,0:T(8,128)S(1)} collective-permute-done((f32[8,48,128]{2,1,0:T(8,128)S(1)}, f32[8,48,128]{2,1,0:T(8,128)S(1)}, u32[]{:S(2)}, u32[]{:S(2)}) %collective-permute-start.1) | collective-permute-done | bytes 196640 | tf_op jit(solution)/shard_map/ppermute | solution.py:34
  20.8 5.1 %collective-permute-done.2.cross = f32[8,48,128]{2,1,0:T(8,128)S(1)} collective-permute-done((f32[8,48,128]{2,1,0:T(8,128)S(1)}, f32[8,48,128]{2,1,0:T(8,128)S(1)}, u32[]{:S(2)}, u32[]{:S(2)}) %collective-permute-start.2) | collective-permute-done | bytes 196640 | tf_op jit(solution)/shard_map/ppermute | solution.py:48
  25.9 3.1 %collective-permute-start.3 = (f32[32,48,128]{2,1,0:T(8,128)S(1)}, f32[32,48,128]{2,1,0:T(8,128)S(1)}, u32[]{:S(2)}, u32[]{:S(2)}) collective-permute-start(f32[32,48,128]{2,1,0:T(8,128)S(1)} %get-tuple-element.20), channel_id=1, source_target_pairs={{0,32},{32,0},{1,33},{33,1},{2,34},{34,2},{3,35},{35,3},{4,36},{36... | collective-permute-start | bytes 2359304 | tf_op jit(solution)/shard_map/ppermute | solution.py:212
  29.1 1.9 %collective-permute-done.3.got_on = f32[32,48,128]{2,1,0:T(8,128)S(1)} collective-permute-done((f32[32,48,128]{2,1,0:T(8,128)S(1)}, f32[32,48,128]{2,1,0:T(8,128)S(1)}, u32[]{:S(2)}, u32[]{:S(2)}) %collective-permute-start.3) | collective-permute-done | bytes 786464 | tf_op jit(solution)/shard_map/ppermute | solution.py:212
  31.0 1.4 %merge.1 = (f32[32,48,128]{2,1,0:T(8,128)S(1)}, f32[32,48,128]{2,1,0:T(8,128)S(1)}) custom-call(s32[16,32]{1,0:T(8,128)S(1)} %copy-done, s32[16,32]{1,0:T(8,128)S(1)} %copy-done.1, f32[32,48,128]{2,1,0:T(8,128)S(1)} %collective-permute-done.3.got_on, f32[128,48,128]{2,1,0:T(8,128)S(1)} %get-tuple-element.21.sums), custom_call_target="tpu_custom_call" | custom-call | tf_op jit(solution)/shard_map/merge/pallas_call | solution.py:213
  32.4 2.5 %collective-permute-start.4 = (f32[32,48,128]{2,1,0:T(8,128)S(1)}, f32[32,48,128]{2,1,0:T(8,128)S(1)}, u32[]{:S(2)}, u32[]{:S(2)}) collective-permute-start(f32[32,48,128]{2,1,0:T(8,128)S(1)} %get-tuple-element.23), channel_id=1, source_target_pairs={{0,4},{4,0},{8,12},{12,8},{16,20},{20,16},{24,28},{28,24},{32,60},... | collective-permute-start | bytes 2359304 | tf_op jit(solution)/shard_map/ppermute | solution.py:34
  34.9 10.5 %collective-permute-start.5 = (f32[8,48,128]{2,1,0:T(8,128)S(1)}, f32[8,48,128]{2,1,0:T(8,128)S(1)}, u32[]{:S(2)}, u32[]{:S(2)}) collective-permute-start(f32[8,48,128]{2,1,0:T(8,128)S(1)} %quarter.1), channel_id=1, source_target_pairs={{32,67},{33,66},{34,65},{35,64},{64,35},{65,34},{66,33},{67,32},{9... | collective-permute-start | bytes 589832 | tf_op jit(solution)/shard_map/ppermute | solution.py:211
  45.4 8.5 %collective-permute-done.5.crossed = f32[8,48,128]{2,1,0:T(8,128)S(1)} collective-permute-done((f32[8,48,128]{2,1,0:T(8,128)S(1)}, f32[8,48,128]{2,1,0:T(8,128)S(1)}, u32[]{:S(2)}, u32[]{:S(2)}) %collective-permute-start.5) | collective-permute-done | bytes 196640 | tf_op jit(solution)/shard_map/ppermute | solution.py:211
  54.0 1.9 %collective-permute-start.6 = (f32[8,48,128]{2,1,0:T(8,128)S(1)}, f32[8,48,128]{2,1,0:T(8,128)S(1)}, u32[]{:S(2)}, u32[]{:S(2)}) collective-permute-start(f32[8,48,128]{2,1,0:T(8,128)S(1)} %collective-permute-done.5.crossed), channel_id=1, source_target_pairs={{0,4},{4,0},{8,12},{12,8},{16,20},{20,16},{24,28},{28,24},{32,60},... | collective-permute-start | bytes 589832 | tf_op jit(solution)/shard_map/ppermute | solution.py:34
  55.9 5.6 %collective-permute-done.6.passed = f32[8,48,128]{2,1,0:T(8,128)S(1)} collective-permute-done((f32[8,48,128]{2,1,0:T(8,128)S(1)}, f32[8,48,128]{2,1,0:T(8,128)S(1)}, u32[]{:S(2)}, u32[]{:S(2)}) %collective-permute-start.6) | collective-permute-done | bytes 196640 | tf_op jit(solution)/shard_map/ppermute | solution.py:34
  61.5 2.0 %place.1 = f32[32,48,128]{2,1,0:T(8,128)} custom-call(s32[16,32]{1,0:T(8,128)S(1)} %copy-done, s32[16,32]{1,0:T(8,128)S(1)} %copy-done.1, f32[32,48,128]{2,1,0:T(8,128)S(1)} %get-tuple-element.22.keep, f32[32,48,128]{2,1,0:T(8,128)S(1)} %collective-permute-done.4.got, f32[8,48,128]{2,1,0:T(8,128)S(1)} %collective-permute-done.5.crossed, ...), custom_call_target="tpu_custom_call" | custom-call | tf_op jit(solution)/shard_map/place/pallas_call | solution.py:223
  63.5 6.1 %all-to-all-start = ((f32[16,1,12288]{2,1,0:T(1,128)}), f32[16,1,12288]{2,1,0:T(1,128)S(1)}, u32[]{:S(2)}, u32[]{:S(2)}) async-start(f32[16,1,12288]{2,1,0:T(1,128)} %bitcast.3), calls=%async_computation | async-start | bytes 1572864 | tf_op jit(solution)/shard_map/all_to_all | solution.py:231
  69.8 0.1 mul.45.matrix
  69.9 0.2 reshape.44.precond
  70.1 0.2 spectral.1.part
  70.3 24.8 %all-to-all-done = f32[16,1,12288]{2,1,0:T(1,128)S(1)} async-done(((f32[16,1,12288]{2,1,0:T(1,128)}), f32[16,1,12288]{2,1,0:T(1,128)S(1)}, u32[]{:S(2)}, u32[]{:S(2)}) %all-to-all-start) | async-done | bytes 786464 | tf_op jit(solution)/shard_map/all_to_all | solution.py:231
  95.1 0.2 last.1
  95.3 0.6 copy.12
  (18 shorter events, 0.2 us)
Async XLA Ops:
  0.0 7.1 %copy-start = (s32[16,32]{1,0:T(8,128)S(1)}, s32[16,32]{1,0:T(8,128)}, u32[]{:S(2)}) copy-start(s32[16,32]{1,0:T(8,128)} %lower.5) | copy-start | bytes 6148
  0.0 7.1 %copy-start.1 = (s32[16,32]{1,0:T(8,128)S(1)}, s32[16,32]{1,0:T(8,128)}, u32[]{:S(2)}) copy-start(s32[16,32]{1,0:T(8,128)} %upper.5) | copy-start | bytes 6148
  0.0 7.1 %copy-start.3 = (s32[2,16]{1,0:T(2,128)S(1)}, s32[2,16]{1,0:T(2,128)}, u32[]{:S(2)}) copy-start(s32[2,16]{1,0:T(2,128)} %columns.1) | copy-start | bytes 388
  8.9 9.7 %collective-permute-start = (f32[8,48,128]{2,1,0:T(8,128)S(1)}, f32[8,48,128]{2,1,0:T(8,128)S(1)}, u32[]{:S(2)}, u32[]{:S(2)}) collective-permute-start(f32[8,48,128]{2,1,0:T(8,128)S(1)} %get-tuple-element.15), channel_id=1, source_target_pairs={{0,1},{1,0},{2,3},{3,2},{4,5},{5,4},{6,7},{7,6},{8,9},{9,8},{10,11... | collective-permute-start | bytes 589832 | tf_op jit(solution)/shard_map/ppermute | solution.py:38
  13.2 7.6 %collective-permute-start.1 = (f32[8,48,128]{2,1,0:T(8,128)S(1)}, f32[8,48,128]{2,1,0:T(8,128)S(1)}, u32[]{:S(2)}, u32[]{:S(2)}) collective-permute-start(f32[8,48,128]{2,1,0:T(8,128)S(1)} %get-tuple-element.16), channel_id=1, source_target_pairs={{0,4},{4,0},{8,12},{12,8},{16,20},{20,16},{24,28},{28,24},{32,60},... | collective-permute-start | bytes 589832 | tf_op jit(solution)/shard_map/ppermute | solution.py:34
  16.7 9.2 %collective-permute-start.2 = (f32[8,48,128]{2,1,0:T(8,128)S(1)}, f32[8,48,128]{2,1,0:T(8,128)S(1)}, u32[]{:S(2)}, u32[]{:S(2)}) collective-permute-start(f32[8,48,128]{2,1,0:T(8,128)S(1)} %get-tuple-element.17), channel_id=1, source_target_pairs={{0,5},{1,4},{4,1},{5,0},{8,13},{9,12},{12,9},{13,8},{16,21},{17,20... | collective-permute-start | bytes 589832 | tf_op jit(solution)/shard_map/ppermute | solution.py:48
  25.9 5.0 %collective-permute-start.3 = (f32[32,48,128]{2,1,0:T(8,128)S(1)}, f32[32,48,128]{2,1,0:T(8,128)S(1)}, u32[]{:S(2)}, u32[]{:S(2)}) collective-permute-start(f32[32,48,128]{2,1,0:T(8,128)S(1)} %get-tuple-element.20), channel_id=1, source_target_pairs={{0,32},{32,0},{1,33},{33,1},{2,34},{34,2},{3,35},{35,3},{4,36},{36... | collective-permute-start | bytes 2359304 | tf_op jit(solution)/shard_map/ppermute | solution.py:212
  32.4 37.5 %copy-start.4 = (bf16[2,36864]{1,0:T(2,128)(2,1)S(1)}, bf16[2,36864]{1,0:T(2,128)(2,1)}, u32[]{:S(2)}) copy-start(bf16[2,36864]{1,0:T(2,128)(2,1)} %param.11) | copy-start | bytes 442372
  32.4 37.7 %copy-start.2 = (f32[2,192]{1,0:T(2,128)S(1)}, f32[2,192]{1,0:T(2,128)}, u32[]{:S(2)}) copy-start(f32[2,192]{1,0:T(2,128)} %rates.1) | copy-start | bytes 4612
  32.4 29.1 %collective-permute-start.4 = (f32[32,48,128]{2,1,0:T(8,128)S(1)}, f32[32,48,128]{2,1,0:T(8,128)S(1)}, u32[]{:S(2)}, u32[]{:S(2)}) collective-permute-start(f32[32,48,128]{2,1,0:T(8,128)S(1)} %get-tuple-element.23), channel_id=1, source_target_pairs={{0,4},{4,0},{8,12},{12,8},{16,20},{20,16},{24,28},{28,24},{32,60},... | collective-permute-start | bytes 2359304 | tf_op jit(solution)/shard_map/ppermute | solution.py:34
  34.9 19.1 %collective-permute-start.5 = (f32[8,48,128]{2,1,0:T(8,128)S(1)}, f32[8,48,128]{2,1,0:T(8,128)S(1)}, u32[]{:S(2)}, u32[]{:S(2)}) collective-permute-start(f32[8,48,128]{2,1,0:T(8,128)S(1)} %quarter.1), channel_id=1, source_target_pairs={{32,67},{33,66},{34,65},{35,64},{64,35},{65,34},{66,33},{67,32},{9... | collective-permute-start | bytes 589832 | tf_op jit(solution)/shard_map/ppermute | solution.py:211
  54.0 7.6 %collective-permute-start.6 = (f32[8,48,128]{2,1,0:T(8,128)S(1)}, f32[8,48,128]{2,1,0:T(8,128)S(1)}, u32[]{:S(2)}, u32[]{:S(2)}) collective-permute-start(f32[8,48,128]{2,1,0:T(8,128)S(1)} %collective-permute-done.5.crossed), channel_id=1, source_target_pairs={{0,4},{4,0},{8,12},{12,8},{16,20},{20,16},{24,28},{28,24},{32,60},... | collective-permute-start | bytes 589832 | tf_op jit(solution)/shard_map/ppermute | solution.py:34
  63.5 31.5 %all-to-all-start = ((f32[16,1,12288]{2,1,0:T(1,128)}), f32[16,1,12288]{2,1,0:T(1,128)S(1)}, u32[]{:S(2)}, u32[]{:S(2)}) async-start(f32[16,1,12288]{2,1,0:T(1,128)} %bitcast.3), calls=%async_computation | async-start | bytes 1572864 | tf_op jit(solution)/shard_map/all_to_all | solution.py:231
where the time goes:
time: 96.4 us; the launch traced here: 95.9 us
  waiting for transfers between devices  48.1 us (50%)
  starting transfers between devices  33.8 us (35%)
  local copies, waits for them, and re-layouts  8.06 us (8%)
  Pallas kernels  5.64 us (6%)
    all_to_all x1, waiting for transfers between devices, shards(): lax.all_to_all(merged.reshape(16, -1), ('yh', 'zq', 'zp'), 0, 0, tiled=True)  24.8 us
    ppermute x1, starting transfers between devices, shards(): lax.ppermute(leaving, ('x', 'zh', 'core', 'zq', 'zp'), off_chip_pairs())  10.5 us
    ppermute x1, waiting for transfers between devices, shards(): lax.ppermute(leaving, ('x', 'zh', 'core', 'zq', 'zp'), off_chip_pairs())  8.52 us
    ppermute x3, starting transfers between devices, to_mate(): return lax.ppermute(value, ('core', 'yh', 'yp'), pairs)  7.87 us
    ppermute x3, waiting for transfers between devices, to_mate(): return lax.ppermute(value, ('core', 'yh', 'yp'), pairs)  7.77 us
    reshape x1, local copies, waits for them, and re-layouts, shards(): jacobian_tiles.reshape(blocks, slots, tile_width, tile_width)  6.28 us
    all_to_all x1, starting transfers between devices, shards(): lax.all_to_all(merged.reshape(16, -1), ('yh', 'zq', 'zp'), 0, 0, tiled=True)  6.08 us
    ppermute x1, waiting for transfers between devices, to_mates_side(): return lax.ppermute(value, ('core', 'yh', 'yp', 'zp'), pairs)  5.08 us
  transfers between devices with their start and end apart: 8, of which 6 were waited for; matrix products, arithmetic and copies ran while one was open for 0% of the time, Pallas kernels for 0%

commit v1 on v0

--- a/solution.py
+++ b/solution.py
@@ -12,6 +12,8 @@
 AXES = ("x", "zh", "core", "yh", "yp", "zq", "zp")
 SIZES = (4, 2, 2, 4, 2, 2, 2)
 PLANES = (48, 128)
+TILE = 192
+LANE_PARTS = ((0, 0), (1, 0), (1, 1), (2, 1))
 KEEP, GIVE, OFF, ON, ROWS = 0, 32, 64, 96, 128
 
 
@@ -69,19 +71,61 @@
     return (block >> 3) & 1
 
 
-def terms_kernel(columns, lower, upper, adj, tiles, sums, own, side, mate, cross, on):
+def spread_adjoint(adj, left):
+    wide = left.shape[1]
+    entry = lax.broadcasted_iota(jnp.int32, (TILE, wide), 0)
+    place = lax.broadcasted_iota(jnp.int32, (TILE, wide), 1)
+    first = (entry >> 1) * 6
+    spread = jnp.where((place >= first) & (place < first + 6), 1.0, 0.0).astype(jnp.bfloat16)
+    column = lax.broadcasted_iota(jnp.int32, (32, TILE), 1)
+    phase = lax.rem(lax.broadcasted_iota(jnp.int32, (32, wide), 1), 6)
+    for b in range(2):
+        for p in range(2):
+            half = jnp.where((column & 1) == p, adj[b].astype(jnp.float32), 0.0)
+            row = jnp.dot(
+                half.astype(jnp.bfloat16), spread, preferred_element_type=jnp.float32
+            )
+            for q, (c, parity) in enumerate(LANE_PARTS):
+                if parity == p:
+                    at = (q * 2 + b) * 32
+                    left[at : at + 32] = jnp.where(phase == 2 * c + b, row, 0.0).astype(
+                        jnp.bfloat16
+                    )
+
+
+def terms_kernel(
+    columns, lower, upper, adj, tiles, ours, own, side, mate, cross, on, sums, left, held, arrived
+):
+    copies = [
+        pltpu.make_async_copy(tiles.at[k], held.at[k], arrived.at[k]) for k in range(17)
+    ]
+    for copy in copies:
+        copy.start()
     odd, mine = lax.axis_index("core"), lax.axis_index("yp")
     quarter = mine * 2 + lax.axis_index("zp")
     off_base = GROUP_BLOCKS + HALO * odd
     on_base = GROUP_BLOCKS + HALO * (1 - odd)
     for i in range(ROWS):
         sums[i] = jnp.zeros(PLANES, jnp.float32)
-    for b in range(2):
-        rows = adj[b]
-        for k in range(17):
-            term = jnp.dot(rows, tiles[k, b], preferred_element_type=jnp.float32)
-            tail = jnp.concatenate([term[:16, 128:], term[16:, 128:]], axis=1)
-            planes = jnp.concatenate([term[:16, :128], term[16:, :128], tail], axis=0)
+    spread_adjoint(adj, left)
+    low = lax.broadcasted_iota(jnp.int32, (32, 128), 1) < 64
+    products = []
+    for some in (range(9), range(9, 17)):
+        for k in some:
+            copies[k].wait()
+        right = jnp.concatenate([held[k] for k in some], axis=1)
+        every = jnp.dot(left[...], right, preferred_element_type=jnp.float32)
+        products += [every[:, 128 * i : 128 * i + 128] for i in range(len(some))]
+    for k in range(17):
+        for b in range(2):
+            t = [products[k][(q * 2 + b) * 32 : (q * 2 + b) * 32 + 32] for q in range(4)]
+            main = t[0] + pltpu.roll(jnp.where(low, t[3], t[2]), 64, 1)
+            tail = jnp.where(
+                low[:16],
+                t[1][:16] + pltpu.roll(t[3][:16], 64, 1),
+                pltpu.roll(t[1][16:], 64, 1) + t[3][16:],
+            )
+            planes = jnp.concatenate([main, tail], axis=0)
             if k == 0:
                 target = lax.axis_index("yh") * 8 + lax.axis_index("zq") * 4 + lax.axis_index("zp") * 2 + b
             else:
@@ -97,6 +141,7 @@
                     ),
                 )
             sums[target] += planes
+    ours[...] = sums[:OFF]
     own[...] = sums[OFF : OFF + 8]
     side[...] = sums[OFF + 8 : OFF + 16]
     mate[...] = sums[OFF + 16 : OFF + 24]
@@ -108,11 +153,11 @@
     leaving[...] = (own[...] + side[...]) + (mate[...] + cross[...])
 
 
-def merge_kernel(lower, upper, got_on, sums, keep, give):
+def merge_kernel(lower, upper, got_on, ours, leaving, keep, give):
     sibling, odd = group_index() ^ 1, lax.axis_index("core")
     mine = lax.axis_index("yp")
-    keep[...] = sums[KEEP : KEEP + 32]
-    give[...] = sums[GIVE : GIVE + 32]
+    keep[...] = ours[KEEP : KEEP + 32]
+    give[...] = ours[GIVE : GIVE + 32]
     for h in range(HALO):
         block = jnp.where(odd == 1, upper[sibling, h], lower[sibling, h])
         same = parity_of(block) == mine
@@ -185,20 +230,31 @@
 def shards(adjoint, jacobian_tiles, columns, cell_rates, precond, lower_list, upper_list):
     blocks, row_count, tile_width = adjoint.shape
     slots = jacobian_tiles.shape[1]
-    tiles = jacobian_tiles.reshape(blocks, slots, tile_width, tile_width).transpose(1, 0, 2, 3)
+    stored = slots, blocks * tile_width * tile_width // 128, 128
+    tiles = jacobian_tiles.reshape(blocks, slots, -1, 128).transpose(1, 2, 0, 3).reshape(stored)
     square_precond = precond.reshape(blocks, tile_width, tile_width)
     padded = jnp.pad(
         adjoint.reshape(blocks, ADJ, INST, tile_width), ((0, 0), (0, 0), (0, 1), (0, 0))
     ).reshape(blocks, 32, tile_width)
 
-    sums, own, side, mate, cross, on = pl.pallas_call(
+    ours, own, side, mate, cross, on = pl.pallas_call(
         terms_kernel,
-        out_shape=stack(ROWS, 8, 8, 8, 8, HALO),
-        in_specs=[scalars(), scalars(), scalars(), whole(), whole()],
+        out_shape=stack(OFF, 8, 8, 8, 8, HALO),
+        in_specs=[scalars(), scalars(), scalars(), whole(), pl.BlockSpec(memory_space=pltpu.HBM)],
         out_specs=[whole()] * 6,
-        compiler_params=pltpu.CompilerParams(vmem_limit_bytes=32 * 2**20),
+        scratch_shapes=[
+            pltpu.VMEM((ROWS,) + PLANES, jnp.float32),
+            pltpu.VMEM((256, stored[1]), jnp.bfloat16),
+            pltpu.VMEM(stored, jnp.bfloat16),
+            pltpu.SemaphoreType.DMA((slots,)),
+        ],
+        compiler_params=pltpu.CompilerParams(vmem_limit_bytes=50 * 2**20),
         name="terms",
     )(columns, lower_list, upper_list, padded, tiles)
+    side = to_side(side)
+    mate = to_mate(mate)
+    cross = to_mates_side(cross)
+    got_on = lax.ppermute(on, "core", [(0, 1), (1, 0)])
     leaving = pl.pallas_call(
         quarter_kernel,
         out_shape=stack(8)[0],
@@ -206,18 +262,16 @@
         out_specs=whole(),
         compiler_params=pltpu.CompilerParams(vmem_limit_bytes=16 * 2**20),
         name="quarter",
-    )(to_side(side), to_mate(mate), to_mates_side(cross), own)
-    leaving, on = lax.optimization_barrier((leaving, on))
+    )(side, mate, cross, own)
     crossed = lax.ppermute(leaving, ("x", "zh", "core", "zq", "zp"), off_chip_pairs())
-    got_on = lax.ppermute(on, "core", [(0, 1), (1, 0)])
     keep, give = pl.pallas_call(
         merge_kernel,
         out_shape=stack(32, 32),
-        in_specs=[scalars(), scalars()] + [whole()] * 2,
+        in_specs=[scalars(), scalars(), whole(), whole(), whole()],
         out_specs=[whole()] * 2,
         compiler_params=pltpu.CompilerParams(vmem_limit_bytes=24 * 2**20),
         name="merge",
-    )(lower_list, upper_list, got_on, sums)
+    )(lower_list, upper_list, got_on, ours, leaving)
     got = to_mate(give)
     passed = to_mate(crossed)
     merged = pl.pallas_call(

time: 96.4 us -> 91.6 us (0.950)
  the two profiles are of different devices: /device:TPU:2 before, /device:TPU:6 now
where the time goes in v1:
time: 91.6 us; the launch traced here: 91.1 us
  waiting for transfers between devices  45.4 us (50%)
  starting transfers between devices  33.6 us (37%)
  Pallas kernels  7.94 us (9%)
  local copies, waits for them, and re-layouts  3.8 us (4%)
    all_to_all x1, waiting for transfers between devices, shards(): lax.all_to_all(merged.reshape(16, -1), ('yh', 'zq', 'zp'), 0, 0, tiled=True)  23.7 us
    ppermute x3, starting transfers between devices, to_mate(): return lax.ppermute(value, ('core', 'yh', 'yp'), pairs)  9.85 us
    ppermute x1, starting transfers between devices, shards(): lax.ppermute(leaving, ('x', 'zh', 'core', 'zq', 'zp'), off_chip_pairs())  9.83 us
    ppermute x1, waiting for transfers between devices, shards(): lax.ppermute(leaving, ('x', 'zh', 'core', 'zq', 'zp'), off_chip_pairs())  9.52 us
    ppermute x3, waiting for transfers between devices, to_mate(): return lax.ppermute(value, ('core', 'yh', 'yp'), pairs)  7.65 us
    all_to_all x1, starting transfers between devices, shards(): lax.all_to_all(merged.reshape(16, -1), ('yh', 'zq', 'zp'), 0, 0, tiled=True)  5.8 us
    ppermute x1, waiting for transfers between devices, to_mates_side(): return lax.ppermute(value, ('core', 'yh', 'yp', 'zp'), pairs)  4.42 us
    ppermute x1, starting transfers between devices, to_side(): return lax.ppermute(value, 'zp', [(0, 1), (1, 0)])  4.27 us
  transfers between devices with their start and end apart: 8, of which 6 were waited for; matrix products, arithmetic and copies ran while one was open for 0% of the time, Pallas kernels for 0%

profile of v1, /device:TPU:6, one launch (start us, length us, event | category | flops | bytes accessed | tf_op | source)
XLA Modules:
  0.0 91.1 jit_solution(10988000880439930810)
XLA Ops:
  0.0 0.8 copy.11
  0.8 0.7 copy-done
  1.5 0.7 copy-done.1
  2.2 0.7 copy-done.3
  2.8 4.1 %terms.1 = (f32[64,48,128]{2,1,0:T(8,128)S(1)}, f32[8,48,128]{2,1,0:T(8,128)S(1)}, f32[8,48,128]{2,1,0:T(8,128)S(1)}, f32[8,48,128]{2,1,0:T(8,128)S(1)}, f32[8,4...) custom-call(s32[2,16]{1,0:T(2,128)S(1)} %copy-done.3, s32[16,32]{1,0:T(8,128)S(1)} %copy-done, s32[16,32]{1,0:T(8,128)S(1)} %copy-done.1, ...), custom_call_target="tpu_custom_call" | custom-call | tf_op jit(solution)/shard_map/terms/pallas_call | solution.py:240
  7.0 1.9 %collective-permute-start = (f32[32,48,128]{2,1,0:T(8,128)S(1)}, f32[32,48,128]{2,1,0:T(8,128)S(1)}, u32[]{:S(2)}, u32[]{:S(2)}) collective-permute-start(f32[32,48,128]{2,1,0:T(8,128)S(1)} %get-tuple-element.13), channel_id=1, source_target_pairs={{0,32},{32,0},{1,33},{33,1},{2,34},{34,2},{3,35},{35,3},{4,36},{36... | collective-permute-start | bytes 2359304 | tf_op jit(solution)/shard_map/ppermute | solution.py:257
  8.9 4.3 %collective-permute-start.1 = (f32[8,48,128]{2,1,0:T(8,128)S(1)}, f32[8,48,128]{2,1,0:T(8,128)S(1)}, u32[]{:S(2)}, u32[]{:S(2)}) collective-permute-start(f32[8,48,128]{2,1,0:T(8,128)S(1)} %get-tuple-element.15), channel_id=1, source_target_pairs={{0,1},{1,0},{2,3},{3,2},{4,5},{5,4},{6,7},{7,6},{8,9},{9,8},{10,11... | collective-permute-start | bytes 589832 | tf_op jit(solution)/shard_map/ppermute | solution.py:40
  13.2 3.5 %collective-permute-start.2 = (f32[8,48,128]{2,1,0:T(8,128)S(1)}, f32[8,48,128]{2,1,0:T(8,128)S(1)}, u32[]{:S(2)}, u32[]{:S(2)}) collective-permute-start(f32[8,48,128]{2,1,0:T(8,128)S(1)} %get-tuple-element.16), channel_id=1, source_target_pairs={{0,4},{4,0},{8,12},{12,8},{16,20},{20,16},{24,28},{28,24},{32,60},... | collective-permute-start | bytes 589832 | tf_op jit(solution)/shard_map/ppermute | solution.py:36
  16.7 1.9 %collective-permute-start.3 = (f32[8,48,128]{2,1,0:T(8,128)S(1)}, f32[8,48,128]{2,1,0:T(8,128)S(1)}, u32[]{:S(2)}, u32[]{:S(2)}) collective-permute-start(f32[8,48,128]{2,1,0:T(8,128)S(1)} %get-tuple-element.17), channel_id=1, source_target_pairs={{0,5},{1,4},{4,1},{5,0},{8,13},{9,12},{12,9},{13,8},{16,21},{17,20... | collective-permute-start | bytes 589832 | tf_op jit(solution)/shard_map/ppermute | solution.py:50
  18.7 2.0 %collective-permute-done.2.mate = f32[8,48,128]{2,1,0:T(8,128)S(1)} collective-permute-done((f32[8,48,128]{2,1,0:T(8,128)S(1)}, f32[8,48,128]{2,1,0:T(8,128)S(1)}, u32[]{:S(2)}, u32[]{:S(2)}) %collective-permute-start.2) | collective-permute-done | bytes 196640 | tf_op jit(solution)/shard_map/ppermute | solution.py:36
  20.7 4.4 %collective-permute-done.3.cross = f32[8,48,128]{2,1,0:T(8,128)S(1)} collective-permute-done((f32[8,48,128]{2,1,0:T(8,128)S(1)}, f32[8,48,128]{2,1,0:T(8,128)S(1)}, u32[]{:S(2)}, u32[]{:S(2)}) %collective-permute-start.3) | collective-permute-done | bytes 196640 | tf_op jit(solution)/shard_map/ppermute | solution.py:50
  25.2 1.4 %merge.1 = (f32[32,48,128]{2,1,0:T(8,128)S(1)}, f32[32,48,128]{2,1,0:T(8,128)S(1)}) custom-call(s32[16,32]{1,0:T(8,128)S(1)} %copy-done, s32[16,32]{1,0:T(8,128)S(1)} %copy-done.1, f32[32,48,128]{2,1,0:T(8,128)S(1)} %collective-permute-done.got_on, f32[64,48,128]{2,1,0:T(8,128)S(1)} %get-tuple-element.14.ours, f32[8,48,128]{2,1,0:T(8,128)S(1)} %quarter.1.leaving), custom_call_target="tpu_custom_call" | custom-call | tf_op jit(solution)/shard_map/merge/pallas_call | solution.py:267
  26.7 4.5 %collective-permute-start.4 = (f32[32,48,128]{2,1,0:T(8,128)S(1)}, f32[32,48,128]{2,1,0:T(8,128)S(1)}, u32[]{:S(2)}, u32[]{:S(2)}) collective-permute-start(f32[32,48,128]{2,1,0:T(8,128)S(1)} %get-tuple-element.20), channel_id=1, source_target_pairs={{0,4},{4,0},{8,12},{12,8},{16,20},{20,16},{24,28},{28,24},{32,60},... | collective-permute-start | bytes 2359304 | tf_op jit(solution)/shard_map/ppermute | solution.py:36
  31.1 9.8 %collective-permute-start.5 = (f32[8,48,128]{2,1,0:T(8,128)S(1)}, f32[8,48,128]{2,1,0:T(8,128)S(1)}, u32[]{:S(2)}, u32[]{:S(2)}) collective-permute-start(f32[8,48,128]{2,1,0:T(8,128)S(1)} %quarter.1.leaving), channel_id=1, source_target_pairs={{32,67},{33,66},{34,65},{35,64},{64,35},{65,34},{66,33},{67,32},{9... | collective-permute-start | bytes 589832 | tf_op jit(solution)/shard_map/ppermute | solution.py:266
  41.0 9.5 %collective-permute-done.5.crossed = f32[8,48,128]{2,1,0:T(8,128)S(1)} collective-permute-done((f32[8,48,128]{2,1,0:T(8,128)S(1)}, f32[8,48,128]{2,1,0:T(8,128)S(1)}, u32[]{:S(2)}, u32[]{:S(2)}) %collective-permute-start.5) | collective-permute-done | bytes 196640 | tf_op jit(solution)/shard_map/ppermute | solution.py:266
  50.5 1.9 %collective-permute-start.6 = (f32[8,48,128]{2,1,0:T(8,128)S(1)}, f32[8,48,128]{2,1,0:T(8,128)S(1)}, u32[]{:S(2)}, u32[]{:S(2)}) collective-permute-start(f32[8,48,128]{2,1,0:T(8,128)S(1)} %collective-permute-done.5.crossed), channel_id=1, source_target_pairs={{0,4},{4,0},{8,12},{12,8},{16,20},{20,16},{24,28},{28,24},{32,60},... | collective-permute-start | bytes 589832 | tf_op jit(solution)/shard_map/ppermute | solution.py:36
  52.4 5.6 %collective-permute-done.6.passed = f32[8,48,128]{2,1,0:T(8,128)S(1)} collective-permute-done((f32[8,48,128]{2,1,0:T(8,128)S(1)}, f32[8,48,128]{2,1,0:T(8,128)S(1)}, u32[]{:S(2)}, u32[]{:S(2)}) %collective-permute-start.6) | collective-permute-done | bytes 196640 | tf_op jit(solution)/shard_map/ppermute | solution.py:36
  58.0 2.0 %place.1 = f32[32,48,128]{2,1,0:T(8,128)} custom-call(s32[16,32]{1,0:T(8,128)S(1)} %copy-done, s32[16,32]{1,0:T(8,128)S(1)} %copy-done.1, f32[32,48,128]{2,1,0:T(8,128)S(1)} %get-tuple-element.19.keep, f32[32,48,128]{2,1,0:T(8,128)S(1)} %collective-permute-done.4.got, f32[8,48,128]{2,1,0:T(8,128)S(1)} %collective-permute-done.5.crossed, ...), custom_call_target="tpu_custom_call" | custom-call | tf_op jit(solution)/shard_map/place/pallas_call | solution.py:277
  60.0 5.8 %all-to-all-start = ((f32[16,1,12288]{2,1,0:T(1,128)}), f32[16,1,12288]{2,1,0:T(1,128)S(1)}, u32[]{:S(2)}, u32[]{:S(2)}) async-start(f32[16,1,12288]{2,1,0:T(1,128)} %bitcast.5), calls=%async_computation | async-start | bytes 1572864 | tf_op jit(solution)/shard_map/all_to_all | solution.py:285
  66.1 0.2 reshape.48.precond
  66.3 0.2 spectral.1.part
  66.5 23.7 %all-to-all-done = f32[16,1,12288]{2,1,0:T(1,128)S(1)} async-done(((f32[16,1,12288]{2,1,0:T(1,128)}), f32[16,1,12288]{2,1,0:T(1,128)S(1)}, u32[]{:S(2)}, u32[]{:S(2)}) %all-to-all-start) | async-done | bytes 786464 | tf_op jit(solution)/shard_map/all_to_all | solution.py:285
  90.2 0.2 last.1
  90.4 0.6 copy.14
  (17 shorter events, 0.4 us)
Async XLA Ops:
  0.8 0.7 copy-start
  1.5 0.7 copy-start.1
  2.2 0.7 copy-start.3
  7.0 18.2 %collective-permute-start = (f32[32,48,128]{2,1,0:T(8,128)S(1)}, f32[32,48,128]{2,1,0:T(8,128)S(1)}, u32[]{:S(2)}, u32[]{:S(2)}) collective-permute-start(f32[32,48,128]{2,1,0:T(8,128)S(1)} %get-tuple-element.13), channel_id=1, source_target_pairs={{0,32},{32,0},{1,33},{33,1},{2,34},{34,2},{3,35},{35,3},{4,36},{36... | collective-permute-start | bytes 2359304 | tf_op jit(solution)/shard_map/ppermute | solution.py:257
  8.9 9.8 %collective-permute-start.1 = (f32[8,48,128]{2,1,0:T(8,128)S(1)}, f32[8,48,128]{2,1,0:T(8,128)S(1)}, u32[]{:S(2)}, u32[]{:S(2)}) collective-permute-start(f32[8,48,128]{2,1,0:T(8,128)S(1)} %get-tuple-element.15), channel_id=1, source_target_pairs={{0,1},{1,0},{2,3},{3,2},{4,5},{5,4},{6,7},{7,6},{8,9},{9,8},{10,11... | collective-permute-start | bytes 589832 | tf_op jit(solution)/shard_map/ppermute | solution.py:40
  13.2 7.6 %collective-permute-start.2 = (f32[8,48,128]{2,1,0:T(8,128)S(1)}, f32[8,48,128]{2,1,0:T(8,128)S(1)}, u32[]{:S(2)}, u32[]{:S(2)}) collective-permute-start(f32[8,48,128]{2,1,0:T(8,128)S(1)} %get-tuple-element.16), channel_id=1, source_target_pairs={{0,4},{4,0},{8,12},{12,8},{16,20},{20,16},{24,28},{28,24},{32,60},... | collective-permute-start | bytes 589832 | tf_op jit(solution)/shard_map/ppermute | solution.py:36
  16.7 8.5 %collective-permute-start.3 = (f32[8,48,128]{2,1,0:T(8,128)S(1)}, f32[8,48,128]{2,1,0:T(8,128)S(1)}, u32[]{:S(2)}, u32[]{:S(2)}) collective-permute-start(f32[8,48,128]{2,1,0:T(8,128)S(1)} %get-tuple-element.17), channel_id=1, source_target_pairs={{0,5},{1,4},{4,1},{5,0},{8,13},{9,12},{12,9},{13,8},{16,21},{17,20... | collective-permute-start | bytes 589832 | tf_op jit(solution)/shard_map/ppermute | solution.py:50
  26.6 39.5 %copy-start.4 = (bf16[2,36864]{1,0:T(2,128)(2,1)S(1)}, bf16[2,36864]{1,0:T(2,128)(2,1)}, u32[]{:S(2)}) copy-start(bf16[2,36864]{1,0:T(2,128)(2,1)} %param.11) | copy-start | bytes 442372
  26.7 39.7 %copy-start.2 = (f32[2,192]{1,0:T(2,128)S(1)}, f32[2,192]{1,0:T(2,128)}, u32[]{:S(2)}) copy-start(f32[2,192]{1,0:T(2,128)} %rates.1) | copy-start | bytes 4612
  26.7 31.4 %collective-permute-start.4 = (f32[32,48,128]{2,1,0:T(8,128)S(1)}, f32[32,48,128]{2,1,0:T(8,128)S(1)}, u32[]{:S(2)}, u32[]{:S(2)}) collective-permute-start(f32[32,48,128]{2,1,0:T(8,128)S(1)} %get-tuple-element.20), channel_id=1, source_target_pairs={{0,4},{4,0},{8,12},{12,8},{16,20},{20,16},{24,28},{28,24},{32,60},... | collective-permute-start | bytes 2359304 | tf_op jit(solution)/shard_map/ppermute | solution.py:36
  31.1 19.4 %collective-permute-start.5 = (f32[8,48,128]{2,1,0:T(8,128)S(1)}, f32[8,48,128]{2,1,0:T(8,128)S(1)}, u32[]{:S(2)}, u32[]{:S(2)}) collective-permute-start(f32[8,48,128]{2,1,0:T(8,128)S(1)} %quarter.1.leaving), channel_id=1, source_target_pairs={{32,67},{33,66},{34,65},{35,64},{64,35},{65,34},{66,33},{67,32},{9... | collective-permute-start | bytes 589832 | tf_op jit(solution)/shard_map/ppermute | solution.py:266
  50.5 7.6 %collective-permute-start.6 = (f32[8,48,128]{2,1,0:T(8,128)S(1)}, f32[8,48,128]{2,1,0:T(8,128)S(1)}, u32[]{:S(2)}, u32[]{:S(2)}) collective-permute-start(f32[8,48,128]{2,1,0:T(8,128)S(1)} %collective-permute-done.5.crossed), channel_id=1, source_target_pairs={{0,4},{4,0},{8,12},{12,8},{16,20},{20,16},{24,28},{28,24},{32,60},... | collective-permute-start | bytes 589832 | tf_op jit(solution)/shard_map/ppermute | solution.py:36
  60.0 30.2 %all-to-all-start = ((f32[16,1,12288]{2,1,0:T(1,128)}), f32[16,1,12288]{2,1,0:T(1,128)S(1)}, u32[]{:S(2)}, u32[]{:S(2)}) async-start(f32[16,1,12288]{2,1,0:T(1,128)} %bitcast.5), calls=%async_computation | async-start | bytes 1572864 | tf_op jit(solution)/shard_map/all_to_all | solution.py:285

commit v2 on v1

--- a/solution.py
+++ b/solution.py
@@ -81,7 +81,7 @@
     phase = lax.rem(lax.broadcasted_iota(jnp.int32, (32, wide), 1), 6)
     for b in range(2):
         for p in range(2):
-            half = jnp.where((column & 1) == p, adj[b].astype(jnp.float32), 0.0)
+            half = jnp.where((column & 1) == p, adj[b], 0.0)
             row = jnp.dot(
                 half.astype(jnp.bfloat16), spread, preferred_element_type=jnp.float32
             )
@@ -94,12 +94,18 @@
 
 
 def terms_kernel(
-    columns, lower, upper, adj, tiles, ours, own, side, mate, cross, on, sums, left, held, arrived
+    columns_in, adj_in, tiles,
+    ours, own, side, mate, cross, on, rows,
+    sums, left, held, adj, columns, arrived, loaded,
 ):
+    small = (
+        pltpu.make_async_copy(adj_in, adj, loaded.at[0]),
+        pltpu.make_async_copy(columns_in, columns, loaded.at[1]),
+    )
     copies = [
         pltpu.make_async_copy(tiles.at[k], held.at[k], arrived.at[k]) for k in range(17)
     ]
-    for copy in copies:
+    for copy in small + tuple(copies):
         copy.start()
     odd, mine = lax.axis_index("core"), lax.axis_index("yp")
     quarter = mine * 2 + lax.axis_index("zp")
@@ -107,7 +113,14 @@
     on_base = GROUP_BLOCKS + HALO * (1 - odd)
     for i in range(ROWS):
         sums[i] = jnp.zeros(PLANES, jnp.float32)
-    spread_adjoint(adj, left)
+    for copy in small:
+        copy.wait()
+    gap = jnp.zeros((1, TILE), jnp.float32)
+    wide = adj[...].astype(jnp.float32)
+    for b in range(2):
+        row = wide[:, b, :]
+        rows[b] = jnp.concatenate([row[:INST], gap, row[INST:], gap], axis=0)
+    spread_adjoint(rows, left)
     low = lax.broadcasted_iota(jnp.int32, (32, 128), 1) < 64
     products = []
     for some in (range(9), range(9, 17)):
@@ -172,29 +185,36 @@
             give[row] += got_on[h]
 
 
-def place_kernel(lower, upper, keep, got, crossed, passed, out):
+def add_slots(lower, upper, source, parity, out):
     group, odd = group_index(), lax.axis_index("core")
-    mine = lax.axis_index("yp")
+    mine, mirrored = lax.axis_index("yp"), 1 - lax.axis_index("zp")
     above = jnp.minimum(group + 1, lower.shape[0] - 1)
     below = jnp.maximum(group - 1, 0)
+    for i in range(8):
+        slot = parity * 16 + mirrored * 8 + i
+        block = jnp.where(odd == 1, lower[above, slot], upper[below, slot])
+        row = row_of(block)
+
+        @pl.when(parity_of(block) == mine)
+        def _():
+            out[row] += source[i]
+
+
+def place_kernel(lower, upper, keep, got, crossed, out):
     out[...] = keep[...] + got[...]
-    mirrored = 1 - lax.axis_index("zp")
-    for i in range(8):
-        for source, parity in ((crossed, mine), (passed, 1 - mine)):
-            slot = parity * 16 + mirrored * 8 + i
-            block = jnp.where(odd == 1, lower[above, slot], upper[below, slot])
-            row = row_of(block)
-
-            @pl.when(parity_of(block) == mine)
-            def _():
-                out[row] += source[i]
+    add_slots(lower, upper, crossed, lax.axis_index("yp"), out)
+
+
+def finish_kernel(lower, upper, part, passed, out):
+    out[...] = part[...]
+    add_slots(lower, upper, passed, 1 - lax.axis_index("yp"), out)
 
 
 def spectral_kernel(matrix, adj, rates, out):
     for b in range(2):
         part = jnp.dot(
             matrix[...],
-            adj[b].astype(jnp.float32),
+            adj[b],
             precision=lax.Precision.HIGHEST,
             preferred_element_type=jnp.float32,
         )
@@ -223,6 +243,10 @@
     return pl.BlockSpec(memory_space=pltpu.SMEM)
 
 
+def in_hbm(*arrays):
+    return [pltpu.with_memory_space_constraint(a, pltpu.HBM) for a in arrays]
+
+
 def stack(*counts):
     return [jax.ShapeDtypeStruct((n,) + PLANES, jnp.float32) for n in counts]
 
@@ -233,24 +257,25 @@
     stored = slots, blocks * tile_width * tile_width // 128, 128
     tiles = jacobian_tiles.reshape(blocks, slots, -1, 128).transpose(1, 2, 0, 3).reshape(stored)
     square_precond = precond.reshape(blocks, tile_width, tile_width)
-    padded = jnp.pad(
-        adjoint.reshape(blocks, ADJ, INST, tile_width), ((0, 0), (0, 0), (0, 1), (0, 0))
-    ).reshape(blocks, 32, tile_width)
-
-    ours, own, side, mate, cross, on = pl.pallas_call(
+
+    ours, own, side, mate, cross, on, rows = pl.pallas_call(
         terms_kernel,
-        out_shape=stack(OFF, 8, 8, 8, 8, HALO),
-        in_specs=[scalars(), scalars(), scalars(), whole(), pl.BlockSpec(memory_space=pltpu.HBM)],
-        out_specs=[whole()] * 6,
+        out_shape=stack(OFF, 8, 8, 8, 8, HALO)
+        + [jax.ShapeDtypeStruct((blocks, 32, tile_width), jnp.float32)],
+        in_specs=[pl.BlockSpec(memory_space=pltpu.HBM)] * 3,
+        out_specs=[whole()] * 7,
         scratch_shapes=[
             pltpu.VMEM((ROWS,) + PLANES, jnp.float32),
             pltpu.VMEM((256, stored[1]), jnp.bfloat16),
             pltpu.VMEM(stored, jnp.bfloat16),
+            pltpu.VMEM((row_count, blocks, tile_width), jnp.bfloat16),
+            pltpu.SMEM(columns.shape, jnp.int32),
             pltpu.SemaphoreType.DMA((slots,)),
+            pltpu.SemaphoreType.DMA((2,)),
         ],
         compiler_params=pltpu.CompilerParams(vmem_limit_bytes=50 * 2**20),
         name="terms",
-    )(columns, lower_list, upper_list, padded, tiles)
+    )(*in_hbm(columns, adjoint.transpose(1, 0, 2), tiles))
     side = to_side(side)
     mate = to_mate(mate)
     cross = to_mates_side(cross)
@@ -274,14 +299,16 @@
     )(lower_list, upper_list, got_on, ours, leaving)
     got = to_mate(give)
     passed = to_mate(crossed)
-    merged = pl.pallas_call(
-        place_kernel,
-        out_shape=stack(32)[0],
-        in_specs=[scalars(), scalars()] + [whole()] * 4,
-        out_specs=whole(),
-        compiler_params=pltpu.CompilerParams(vmem_limit_bytes=16 * 2**20),
-        name="place",
-    )(lower_list, upper_list, keep, got, crossed, passed)
+    merged = keep
+    for kernel, arrays in ((place_kernel, (got, crossed)), (finish_kernel, (passed,))):
+        merged = pl.pallas_call(
+            kernel,
+            out_shape=stack(32)[0],
+            in_specs=[scalars(), scalars()] + [whole()] * (1 + len(arrays)),
+            out_specs=whole(),
+            compiler_params=pltpu.CompilerParams(vmem_limit_bytes=16 * 2**20),
+            cost_estimate=pl.CostEstimate(flops=2**20, bytes_accessed=2**22, transcendentals=0),
+        )(lower_list, upper_list, merged, *arrays)
     shared = lax.all_to_all(merged.reshape(16, -1), ("yh", "zq", "zp"), 0, 0, tiled=True)
 
     half = jnp.pad(spectral_matrix(INST).T, ((0, 1), (0, 1)))
@@ -293,7 +320,7 @@
         out_specs=whole(),
         compiler_params=pltpu.CompilerParams(vmem_limit_bytes=8 * 2**20),
         name="spectral",
-    )(matrix, padded, cell_rates)
+    )(matrix, rows, cell_rates)
     result = pl.pallas_call(
         last_kernel,
         out_shape=jax.ShapeDtypeStruct((blocks, 32, tile_width), jnp.bfloat16),

time: 91.6 us -> 87.9 us (0.960)
  local copies, waits for them, and re-layouts: 3.8 us -> 0.97 us
  waiting for transfers between devices: 45.4 us -> 44.4 us
    unnamed x10 -> x8, local copies, waits for them, and re-layouts: 2.08 us -> 0.02 us
    ppermute x3, waiting for transfers between devices: 7.65 us -> 6.63 us  [to_mate(): return lax.ppermute(value, ('core', 'yh', 'yp'), pairs)]
    pallas_call x2 -> x3, Pallas kernels: 6.09 us -> 6.54 us  [the longest x1 3.71 us: shards(): pl.pallas_call(terms_kernel, out_shape=stack(OFF, 8, 8, 8, 8, HALO) + [ja...]
  transfers between devices with their start and end apart: 8 -> 8, of which waited for: 6 -> 6; matrix products, arithmetic and copies ran while one was open for 0% -> 1% of each run, Pallas kernels for 0% -> 1%
where the time goes in v2:
time: 87.9 us; the launch traced here: 87.5 us
  waiting for transfers between devices  44.4 us (51%)
  starting transfers between devices  33.4 us (38%)
  Pallas kernels  8.39 us (10%)
  local copies, waits for them, and re-layouts  0.97 us (1%)
    all_to_all x1, waiting for transfers between devices, shards(): lax.all_to_all(merged.reshape(16, -1), ('yh', 'zq', 'zp'), 0, 0, tiled=True)  23.6 us
    ppermute x1, starting transfers between devices, shards(): lax.ppermute(leaving, ('x', 'zh', 'core', 'zq', 'zp'), off_chip_pairs())  9.81 us
    ppermute x3, starting transfers between devices, to_mate(): return lax.ppermute(value, ('core', 'yh', 'yp'), pairs)  9.72 us
    ppermute x1, waiting for transfers between devices, shards(): lax.ppermute(leaving, ('x', 'zh', 'core', 'zq', 'zp'), off_chip_pairs())  9.54 us
    ppermute x3, waiting for transfers between devices, to_mate(): return lax.ppermute(value, ('core', 'yh', 'yp'), pairs)  6.63 us
    all_to_all x1, starting transfers between devices, shards(): lax.all_to_all(merged.reshape(16, -1), ('yh', 'zq', 'zp'), 0, 0, tiled=True)  5.76 us
    ppermute x1, waiting for transfers between devices, to_mates_side(): return lax.ppermute(value, ('core', 'yh', 'yp', 'zp'), pairs)  4.43 us
    ppermute x1, starting transfers between devices, to_side(): return lax.ppermute(value, 'zp', [(0, 1), (1, 0)])  4.28 us
  transfers between devices with their start and end apart: 8, of which 6 were waited for; matrix products, arithmetic and copies ran while one was open for 1% of the time, Pallas kernels for 1%

profile of v2, /device:TPU:6, one launch (start us, length us, event | category | flops | bytes accessed | tf_op | source)
XLA Modules:
  0.0 87.5 jit_solution(14790865237310728511)
XLA Ops:
  0.0 3.7 %terms.1 = (f32[64,48,128]{2,1,0:T(8,128)S(1)}, f32[8,48,128]{2,1,0:T(8,128)S(1)}, f32[8,48,128]{2,1,0:T(8,128)S(1)}, f32[8,48,128]{2,1,0:T(8,128)S(1)}, f32[8,4...) custom-call(s32[2,16]{1,0:T(2,128)} %columns_in.1, bf16[30,2,192]{2,1,0:T(2,128)(2,1)} %bitcast.14, ...), custom_call_target="tpu_custom_call" | custom-call | tf_op jit(solution)/shard_map/terms/pallas_call | solution.py:261
  3.7 1.9 %collective-permute-start = (f32[32,48,128]{2,1,0:T(8,128)S(1)}, f32[32,48,128]{2,1,0:T(8,128)S(1)}, u32[]{:S(2)}, u32[]{:S(2)}) collective-permute-start(f32[32,48,128]{2,1,0:T(8,128)S(1)} %get-tuple-element.14), channel_id=1, source_target_pairs={{0,32},{32,0},{1,33},{33,1},{2,34},{34,2},{3,35},{35,3},{4,36},{36... | collective-permute-start | bytes 2359304 | tf_op jit(solution)/shard_map/ppermute | solution.py:282
  5.6 4.3 %collective-permute-start.1 = (f32[8,48,128]{2,1,0:T(8,128)S(1)}, f32[8,48,128]{2,1,0:T(8,128)S(1)}, u32[]{:S(2)}, u32[]{:S(2)}) collective-permute-start(f32[8,48,128]{2,1,0:T(8,128)S(1)} %get-tuple-element.16), channel_id=1, source_target_pairs={{0,1},{1,0},{2,3},{3,2},{4,5},{5,4},{6,7},{7,6},{8,9},{9,8},{10,11... | collective-permute-start | bytes 589832 | tf_op jit(solution)/shard_map/ppermute | solution.py:40
  9.9 3.5 %collective-permute-start.2 = (f32[8,48,128]{2,1,0:T(8,128)S(1)}, f32[8,48,128]{2,1,0:T(8,128)S(1)}, u32[]{:S(2)}, u32[]{:S(2)}) collective-permute-start(f32[8,48,128]{2,1,0:T(8,128)S(1)} %get-tuple-element.17), channel_id=1, source_target_pairs={{0,4},{4,0},{8,12},{12,8},{16,20},{20,16},{24,28},{28,24},{32,60},... | collective-permute-start | bytes 589832 | tf_op jit(solution)/shard_map/ppermute | solution.py:36
  13.4 1.9 %collective-permute-start.3 = (f32[8,48,128]{2,1,0:T(8,128)S(1)}, f32[8,48,128]{2,1,0:T(8,128)S(1)}, u32[]{:S(2)}, u32[]{:S(2)}) collective-permute-start(f32[8,48,128]{2,1,0:T(8,128)S(1)} %get-tuple-element.18), channel_id=1, source_target_pairs={{0,5},{1,4},{4,1},{5,0},{8,13},{9,12},{12,9},{13,8},{16,21},{17,20... | collective-permute-start | bytes 589832 | tf_op jit(solution)/shard_map/ppermute | solution.py:50
  15.4 0.1 collective-permute-done.1.side
  15.5 2.0 %collective-permute-done.2.mate = f32[8,48,128]{2,1,0:T(8,128)S(1)} collective-permute-done((f32[8,48,128]{2,1,0:T(8,128)S(1)}, f32[8,48,128]{2,1,0:T(8,128)S(1)}, u32[]{:S(2)}, u32[]{:S(2)}) %collective-permute-start.2) | collective-permute-done | bytes 196640 | tf_op jit(solution)/shard_map/ppermute | solution.py:36
  17.5 4.4 %collective-permute-done.3.cross = f32[8,48,128]{2,1,0:T(8,128)S(1)} collective-permute-done((f32[8,48,128]{2,1,0:T(8,128)S(1)}, f32[8,48,128]{2,1,0:T(8,128)S(1)}, u32[]{:S(2)}, u32[]{:S(2)}) %collective-permute-start.3) | collective-permute-done | bytes 196640 | tf_op jit(solution)/shard_map/ppermute | solution.py:50
  22.0 1.4 %merge.1 = (f32[32,48,128]{2,1,0:T(8,128)S(1)}, f32[32,48,128]{2,1,0:T(8,128)S(1)}) custom-call(s32[16,32]{1,0:T(8,128)S(1)} %copy-done, s32[16,32]{1,0:T(8,128)S(1)} %copy-done.1, f32[32,48,128]{2,1,0:T(8,128)S(1)} %collective-permute-done.got_on, f32[64,48,128]{2,1,0:T(8,128)S(1)} %get-tuple-element.15.ours, f32[8,48,128]{2,1,0:T(8,128)S(1)} %quarter.1.leaving), custom_call_target="tpu_custom_call" | custom-call | tf_op jit(solution)/shard_map/merge/pallas_call | solution.py:292
  23.4 4.3 %collective-permute-start.4 = (f32[32,48,128]{2,1,0:T(8,128)S(1)}, f32[32,48,128]{2,1,0:T(8,128)S(1)}, u32[]{:S(2)}, u32[]{:S(2)}) collective-permute-start(f32[32,48,128]{2,1,0:T(8,128)S(1)} %get-tuple-element.21), channel_id=1, source_target_pairs={{0,4},{4,0},{8,12},{12,8},{16,20},{20,16},{24,28},{28,24},{32,60},... | collective-permute-start | bytes 2359304 | tf_op jit(solution)/shard_map/ppermute | solution.py:36
  27.8 9.8 %collective-permute-start.5 = (f32[8,48,128]{2,1,0:T(8,128)S(1)}, f32[8,48,128]{2,1,0:T(8,128)S(1)}, u32[]{:S(2)}, u32[]{:S(2)}) collective-permute-start(f32[8,48,128]{2,1,0:T(8,128)S(1)} %quarter.1.leaving), channel_id=1, source_target_pairs={{32,67},{33,66},{34,65},{35,64},{64,35},{65,34},{66,33},{67,32},{9... | collective-permute-start | bytes 589832 | tf_op jit(solution)/shard_map/ppermute | solution.py:291
  37.6 9.5 %collective-permute-done.5.crossed = f32[8,48,128]{2,1,0:T(8,128)S(1)} collective-permute-done((f32[8,48,128]{2,1,0:T(8,128)S(1)}, f32[8,48,128]{2,1,0:T(8,128)S(1)}, u32[]{:S(2)}, u32[]{:S(2)}) %collective-permute-start.5) | collective-permute-done | bytes 196640 | tf_op jit(solution)/shard_map/ppermute | solution.py:291
  47.2 1.9 %collective-permute-start.6 = (f32[8,48,128]{2,1,0:T(8,128)S(1)}, f32[8,48,128]{2,1,0:T(8,128)S(1)}, u32[]{:S(2)}, u32[]{:S(2)}) collective-permute-start(f32[8,48,128]{2,1,0:T(8,128)S(1)} %collective-permute-done.5.crossed), channel_id=1, source_target_pairs={{0,4},{4,0},{8,12},{12,8},{16,20},{20,16},{24,28},{28,24},{32,60},... | collective-permute-start | bytes 589832 | tf_op jit(solution)/shard_map/ppermute | solution.py:36
  49.1 1.0 %shard_map.73.part = f32[32,48,128]{2,1,0:T(8,128)S(1)} custom-call(s32[16,32]{1,0:T(8,128)S(1)} %copy-done, s32[16,32]{1,0:T(8,128)S(1)} %copy-done.1, f32[32,48,128]{2,1,0:T(8,128)S(1)} %get-tuple-element.20.keep, f32[32,48,128]{2,1,0:T(8,128)S(1)} %collective-permute-done.4.got, f32[8,48,128]{2,1,0:T(8,128)S(1)} %collective-permute-done.5.crossed), custom_call_target="tpu_custom_call" | custom-call | flops 1048576 | bytes 4194304 | tf_op jit(solution)/shard_map/pallas_call | solution.py:304
  50.1 4.6 %collective-permute-done.6.passed = f32[8,48,128]{2,1,0:T(8,128)S(1)} collective-permute-done((f32[8,48,128]{2,1,0:T(8,128)S(1)}, f32[8,48,128]{2,1,0:T(8,128)S(1)}, u32[]{:S(2)}, u32[]{:S(2)}) %collective-permute-start.6) | collective-permute-done | bytes 196640 | tf_op jit(solution)/shard_map/ppermute | solution.py:36
  54.7 1.9 %shard_map.74 = f32[32,48,128]{2,1,0:T(8,128)} custom-call(s32[16,32]{1,0:T(8,128)S(1)} %copy-done, s32[16,32]{1,0:T(8,128)S(1)} %copy-done.1, f32[32,48,128]{2,1,0:T(8,128)S(1)} %shard_map.73.part, f32[8,48,128]{2,1,0:T(8,128)S(1)} %collective-permute-done.6.passed), custom_call_target="tpu_custom_call" | custom-call | flops 1048576 | bytes 4194304 | tf_op jit(solution)/shard_map/pallas_call | solution.py:304
  56.6 5.8 %all-to-all-start = ((f32[16,1,12288]{2,1,0:T(1,128)}), f32[16,1,12288]{2,1,0:T(1,128)S(1)}, u32[]{:S(2)}, u32[]{:S(2)}) async-start(f32[16,1,12288]{2,1,0:T(1,128)} %bitcast.4), calls=%async_computation | async-start | bytes 1572864 | tf_op jit(solution)/shard_map/all_to_all | solution.py:312
  62.4 0.1 broadcast_multiply_fusion
  62.5 0.1 mul.45.matrix
  62.6 0.2 reshape.40.precond
  62.8 0.2 spectral.1.part
  63.0 23.6 %all-to-all-done = f32[16,1,12288]{2,1,0:T(1,128)S(1)} async-done(((f32[16,1,12288]{2,1,0:T(1,128)}), f32[16,1,12288]{2,1,0:T(1,128)S(1)}, u32[]{:S(2)}, u32[]{:S(2)}) %all-to-all-start) | async-done | bytes 786464 | tf_op jit(solution)/shard_map/all_to_all | solution.py:312
  86.6 0.2 last.1
  86.8 0.6 copy.12
  (14 shorter events, 0.1 us)
Async XLA Ops:
  0.0 22.0 %copy-start = (s32[16,32]{1,0:T(8,128)S(1)}, s32[16,32]{1,0:T(8,128)}, u32[]{:S(2)}) copy-start(s32[16,32]{1,0:T(8,128)} %lower.5) | copy-start | bytes 6148
  0.0 22.0 %copy-start.1 = (s32[16,32]{1,0:T(8,128)S(1)}, s32[16,32]{1,0:T(8,128)}, u32[]{:S(2)}) copy-start(s32[16,32]{1,0:T(8,128)} %upper.5) | copy-start | bytes 6148
  3.7 18.3 %collective-permute-start = (f32[32,48,128]{2,1,0:T(8,128)S(1)}, f32[32,48,128]{2,1,0:T(8,128)S(1)}, u32[]{:S(2)}, u32[]{:S(2)}) collective-permute-start(f32[32,48,128]{2,1,0:T(8,128)S(1)} %get-tuple-element.14), channel_id=1, source_target_pairs={{0,32},{32,0},{1,33},{33,1},{2,34},{34,2},{3,35},{35,3},{4,36},{36... | collective-permute-start | bytes 2359304 | tf_op jit(solution)/shard_map/ppermute | solution.py:282
  5.6 9.8 %collective-permute-start.1 = (f32[8,48,128]{2,1,0:T(8,128)S(1)}, f32[8,48,128]{2,1,0:T(8,128)S(1)}, u32[]{:S(2)}, u32[]{:S(2)}) collective-permute-start(f32[8,48,128]{2,1,0:T(8,128)S(1)} %get-tuple-element.16), channel_id=1, source_target_pairs={{0,1},{1,0},{2,3},{3,2},{4,5},{5,4},{6,7},{7,6},{8,9},{9,8},{10,11... | collective-permute-start | bytes 589832 | tf_op jit(solution)/shard_map/ppermute | solution.py:40
  9.9 7.6 %collective-permute-start.2 = (f32[8,48,128]{2,1,0:T(8,128)S(1)}, f32[8,48,128]{2,1,0:T(8,128)S(1)}, u32[]{:S(2)}, u32[]{:S(2)}) collective-permute-start(f32[8,48,128]{2,1,0:T(8,128)S(1)} %get-tuple-element.17), channel_id=1, source_target_pairs={{0,4},{4,0},{8,12},{12,8},{16,20},{20,16},{24,28},{28,24},{32,60},... | collective-permute-start | bytes 589832 | tf_op jit(solution)/shard_map/ppermute | solution.py:36
  13.4 8.5 %collective-permute-start.3 = (f32[8,48,128]{2,1,0:T(8,128)S(1)}, f32[8,48,128]{2,1,0:T(8,128)S(1)}, u32[]{:S(2)}, u32[]{:S(2)}) collective-permute-start(f32[8,48,128]{2,1,0:T(8,128)S(1)} %get-tuple-element.18), channel_id=1, source_target_pairs={{0,5},{1,4},{4,1},{5,0},{8,13},{9,12},{12,9},{13,8},{16,21},{17,20... | collective-permute-start | bytes 589832 | tf_op jit(solution)/shard_map/ppermute | solution.py:50
  23.4 25.6 %collective-permute-start.4 = (f32[32,48,128]{2,1,0:T(8,128)S(1)}, f32[32,48,128]{2,1,0:T(8,128)S(1)}, u32[]{:S(2)}, u32[]{:S(2)}) collective-permute-start(f32[32,48,128]{2,1,0:T(8,128)S(1)} %get-tuple-element.21), channel_id=1, source_target_pairs={{0,4},{4,0},{8,12},{12,8},{16,20},{20,16},{24,28},{28,24},{32,60},... | collective-permute-start | bytes 2359304 | tf_op jit(solution)/shard_map/ppermute | solution.py:36
  27.8 19.4 %collective-permute-start.5 = (f32[8,48,128]{2,1,0:T(8,128)S(1)}, f32[8,48,128]{2,1,0:T(8,128)S(1)}, u32[]{:S(2)}, u32[]{:S(2)}) collective-permute-start(f32[8,48,128]{2,1,0:T(8,128)S(1)} %quarter.1.leaving), channel_id=1, source_target_pairs={{32,67},{33,66},{34,65},{35,64},{64,35},{65,34},{66,33},{67,32},{9... | collective-permute-start | bytes 589832 | tf_op jit(solution)/shard_map/ppermute | solution.py:291
  47.2 7.6 %collective-permute-start.6 = (f32[8,48,128]{2,1,0:T(8,128)S(1)}, f32[8,48,128]{2,1,0:T(8,128)S(1)}, u32[]{:S(2)}, u32[]{:S(2)}) collective-permute-start(f32[8,48,128]{2,1,0:T(8,128)S(1)} %collective-permute-done.5.crossed), channel_id=1, source_target_pairs={{0,4},{4,0},{8,12},{12,8},{16,20},{20,16},{24,28},{28,24},{32,60},... | collective-permute-start | bytes 589832 | tf_op jit(solution)/shard_map/ppermute | solution.py:36
  49.1 13.5 %copy-start.3 = (bf16[2,36864]{1,0:T(2,128)(2,1)S(1)}, bf16[2,36864]{1,0:T(2,128)(2,1)}, u32[]{:S(2)}) copy-start(bf16[2,36864]{1,0:T(2,128)(2,1)} %param.11) | copy-start | bytes 442372
  50.1 12.7 %copy-start.2 = (f32[2,192]{1,0:T(2,128)S(1)}, f32[2,192]{1,0:T(2,128)}, u32[]{:S(2)}) copy-start(f32[2,192]{1,0:T(2,128)} %rates.1) | copy-start | bytes 4612
  56.6 30.1 %all-to-all-start = ((f32[16,1,12288]{2,1,0:T(1,128)}), f32[16,1,12288]{2,1,0:T(1,128)S(1)}, u32[]{:S(2)}, u32[]{:S(2)}) async-start(f32[16,1,12288]{2,1,0:T(1,128)} %bitcast.4), calls=%async_computation | async-start | bytes 1572864 | tf_op jit(solution)/shard_map/all_to_all | solution.py:312

commit v3 on v2

--- a/solution.py
+++ b/solution.py
@@ -64,7 +64,7 @@
 
 
 def row_of(block):
-    return ((block >> 4) << 3) + (block & 7)
+    return (((block >> 1) & 3) << 3) + ((block >> 4) << 1) + (block & 1)
 
 
 def parity_of(block):
@@ -140,7 +140,7 @@
             )
             planes = jnp.concatenate([main, tail], axis=0)
             if k == 0:
-                target = lax.axis_index("yh") * 8 + lax.axis_index("zq") * 4 + lax.axis_index("zp") * 2 + b
+                target = lax.axis_index("zq") * 16 + lax.axis_index("zp") * 8 + lax.axis_index("yh") * 2 + b
             else:
                 c = columns[b, k - 1]
                 slot = c - off_base
@@ -200,13 +200,13 @@
             out[row] += source[i]
 
 
-def place_kernel(lower, upper, keep, got, crossed, out):
-    out[...] = keep[...] + got[...]
+def place_kernel(lower, upper, keep, crossed, out):
+    out[...] = keep[...]
     add_slots(lower, upper, crossed, lax.axis_index("yp"), out)
 
 
-def finish_kernel(lower, upper, part, passed, out):
-    out[...] = part[...]
+def finish_kernel(lower, upper, part, got, passed, out):
+    out[...] = part[...] + got[...]
     add_slots(lower, upper, passed, 1 - lax.axis_index("yp"), out)
 
 
@@ -222,6 +222,7 @@
 
 
 def last_kernel(shared, part, precond, out):
+    results = []
     for b in range(2):
         total = shared[0, b]
         for i in range(1, 16):
@@ -230,9 +231,9 @@
         top = jnp.concatenate([total[:16], tail[:, :64]], axis=1)
         bottom = jnp.concatenate([total[16:32], tail[:, 64:]], axis=1)
         combined = (jnp.concatenate([top, bottom], axis=0) + part[b]).astype(jnp.bfloat16)
-        out[b] = jnp.dot(combined, precond[b], preferred_element_type=jnp.float32).astype(
-            jnp.bfloat16
-        )
+        result = jnp.dot(combined, precond[b], preferred_element_type=jnp.float32)
+        results.append(jnp.concatenate([result[:INST], result[16 : 16 + INST]], axis=0))
+    out[...] = jnp.stack(results, axis=1).astype(jnp.bfloat16)
 
 
 def whole():
@@ -300,7 +301,7 @@
     got = to_mate(give)
     passed = to_mate(crossed)
     merged = keep
-    for kernel, arrays in ((place_kernel, (got, crossed)), (finish_kernel, (passed,))):
+    for kernel, arrays in ((place_kernel, (crossed,)), (finish_kernel, (got, passed))):
         merged = pl.pallas_call(
             kernel,
             out_shape=stack(32)[0],
@@ -309,7 +310,7 @@
             compiler_params=pltpu.CompilerParams(vmem_limit_bytes=16 * 2**20),
             cost_estimate=pl.CostEstimate(flops=2**20, bytes_accessed=2**22, transcendentals=0),
         )(lower_list, upper_list, merged, *arrays)
-    shared = lax.all_to_all(merged.reshape(16, -1), ("yh", "zq", "zp"), 0, 0, tiled=True)
+    shared = lax.all_to_all(merged.reshape(16, -1), ("zq", "zp", "yh"), 0, 0, tiled=True)
 
     half = jnp.pad(spectral_matrix(INST).T, ((0, 1), (0, 1)))
     matrix = jnp.kron(jnp.eye(ADJ, dtype=jnp.float32), half)
@@ -323,16 +324,13 @@
     )(matrix, rows, cell_rates)
     result = pl.pallas_call(
         last_kernel,
-        out_shape=jax.ShapeDtypeStruct((blocks, 32, tile_width), jnp.bfloat16),
+        out_shape=jax.ShapeDtypeStruct((row_count, blocks, tile_width), jnp.bfloat16),
         in_specs=[whole()] * 3,
         out_specs=whole(),
         compiler_params=pltpu.CompilerParams(vmem_limit_bytes=8 * 2**20),
         name="last",
     )(shared.reshape(16, blocks, *PLANES), part, square_precond)
-    return (
-        result.reshape(blocks, ADJ, 16, tile_width)[:, :, :INST]
-        .reshape(blocks, row_count, tile_width)
-    )
+    return result.transpose(1, 0, 2)
 
 
 def solution(mesh):

time: 87.9 us -> 89.8 us (1.022)
  waiting for transfers between devices: 44.4 us -> 45.6 us
    all_to_all x1, waiting for transfers between devices: 23.6 us -> 24.8 us  [shards(): lax.all_to_all(merged.reshape(16, -1), ('zq', 'zp', 'yh'), 0, 0, tiled=True)]
  transfers between devices with their start and end apart: 8 -> 8, of which waited for: 6 -> 6; matrix products, arithmetic and copies ran while one was open for 1% -> 0% of each run, Pallas kernels for 1% -> 1%
where the time goes in v3:
time: 89.8 us; the launch traced here: 88.8 us
  waiting for transfers between devices  45.6 us (51%)
  starting transfers between devices  33.4 us (37%)
  Pallas kernels  9.11 us (10%)
    all_to_all x1, waiting for transfers between devices, shards(): lax.all_to_all(merged.reshape(16, -1), ('zq', 'zp', 'yh'), 0, 0, tiled=True)  24.8 us
    ppermute x1, starting transfers between devices, shards(): lax.ppermute(leaving, ('x', 'zh', 'core', 'zq', 'zp'), off_chip_pairs())  9.82 us
    ppermute x3, starting transfers between devices, to_mate(): return lax.ppermute(value, ('core', 'yh', 'yp'), pairs)  9.72 us
    ppermute x1, waiting for transfers between devices, shards(): lax.ppermute(leaving, ('x', 'zh', 'core', 'zq', 'zp'), off_chip_pairs())  9.54 us
    ppermute x3, waiting for transfers between devices, to_mate(): return lax.ppermute(value, ('core', 'yh', 'yp'), pairs)  6.67 us
    all_to_all x1, starting transfers between devices, shards(): lax.all_to_all(merged.reshape(16, -1), ('zq', 'zp', 'yh'), 0, 0, tiled=True)  5.76 us
    ppermute x1, waiting for transfers between devices, to_mates_side(): return lax.ppermute(value, ('core', 'yh', 'yp', 'zp'), pairs)  4.43 us
    ppermute x1, starting transfers between devices, to_side(): return lax.ppermute(value, 'zp', [(0, 1), (1, 0)])  4.28 us
  transfers between devices with their start and end apart: 8, of which 6 were waited for; matrix products, arithmetic and copies ran while one was open for 0% of the time, Pallas kernels for 1%

profile of v3, /device:TPU:6, one launch (start us, length us, event | category | flops | bytes accessed | tf_op | source)
XLA Modules:
  0.0 88.8 jit_solution(2723976778448593344)
XLA Ops:
  0.0 3.7 %terms.1 = (f32[64,48,128]{2,1,0:T(8,128)S(1)}, f32[8,48,128]{2,1,0:T(8,128)S(1)}, f32[8,48,128]{2,1,0:T(8,128)S(1)}, f32[8,48,128]{2,1,0:T(8,128)S(1)}, f32[8,4...) custom-call(s32[2,16]{1,0:T(2,128)} %columns_in.1, bf16[30,2,192]{2,1,0:T(2,128)(2,1)} %bitcast.11, ...), custom_call_target="tpu_custom_call" | custom-call | tf_op jit(solution)/shard_map/terms/pallas_call | solution.py:262
  3.7 1.9 %collective-permute-start = (f32[32,48,128]{2,1,0:T(8,128)S(1)}, f32[32,48,128]{2,1,0:T(8,128)S(1)}, u32[]{:S(2)}, u32[]{:S(2)}) collective-permute-start(f32[32,48,128]{2,1,0:T(8,128)S(1)} %get-tuple-element.14), channel_id=1, source_target_pairs={{0,32},{32,0},{1,33},{33,1},{2,34},{34,2},{3,35},{35,3},{4,36},{36... | collective-permute-start | bytes 2359304 | tf_op jit(solution)/shard_map/ppermute | solution.py:283
  5.7 4.3 %collective-permute-start.1 = (f32[8,48,128]{2,1,0:T(8,128)S(1)}, f32[8,48,128]{2,1,0:T(8,128)S(1)}, u32[]{:S(2)}, u32[]{:S(2)}) collective-permute-start(f32[8,48,128]{2,1,0:T(8,128)S(1)} %get-tuple-element.16), channel_id=1, source_target_pairs={{0,1},{1,0},{2,3},{3,2},{4,5},{5,4},{6,7},{7,6},{8,9},{9,8},{10,11... | collective-permute-start | bytes 589832 | tf_op jit(solution)/shard_map/ppermute | solution.py:40
  10.0 3.5 %collective-permute-start.2 = (f32[8,48,128]{2,1,0:T(8,128)S(1)}, f32[8,48,128]{2,1,0:T(8,128)S(1)}, u32[]{:S(2)}, u32[]{:S(2)}) collective-permute-start(f32[8,48,128]{2,1,0:T(8,128)S(1)} %get-tuple-element.17), channel_id=1, source_target_pairs={{0,4},{4,0},{8,12},{12,8},{16,20},{20,16},{24,28},{28,24},{32,60},... | collective-permute-start | bytes 589832 | tf_op jit(solution)/shard_map/ppermute | solution.py:36
  13.5 1.9 %collective-permute-start.3 = (f32[8,48,128]{2,1,0:T(8,128)S(1)}, f32[8,48,128]{2,1,0:T(8,128)S(1)}, u32[]{:S(2)}, u32[]{:S(2)}) collective-permute-start(f32[8,48,128]{2,1,0:T(8,128)S(1)} %get-tuple-element.18), channel_id=1, source_target_pairs={{0,5},{1,4},{4,1},{5,0},{8,13},{9,12},{12,9},{13,8},{16,21},{17,20... | collective-permute-start | bytes 589832 | tf_op jit(solution)/shard_map/ppermute | solution.py:50
  15.4 0.1 collective-permute-done.1.side
  15.5 2.0 %collective-permute-done.2.mate = f32[8,48,128]{2,1,0:T(8,128)S(1)} collective-permute-done((f32[8,48,128]{2,1,0:T(8,128)S(1)}, f32[8,48,128]{2,1,0:T(8,128)S(1)}, u32[]{:S(2)}, u32[]{:S(2)}) %collective-permute-start.2) | collective-permute-done | bytes 196640 | tf_op jit(solution)/shard_map/ppermute | solution.py:36
  17.5 4.4 %collective-permute-done.3.cross = f32[8,48,128]{2,1,0:T(8,128)S(1)} collective-permute-done((f32[8,48,128]{2,1,0:T(8,128)S(1)}, f32[8,48,128]{2,1,0:T(8,128)S(1)}, u32[]{:S(2)}, u32[]{:S(2)}) %collective-permute-start.3) | collective-permute-done | bytes 196640 | tf_op jit(solution)/shard_map/ppermute | solution.py:50
  22.0 1.5 %merge.1 = (f32[32,48,128]{2,1,0:T(8,128)S(1)}, f32[32,48,128]{2,1,0:T(8,128)S(1)}) custom-call(s32[16,32]{1,0:T(8,128)S(1)} %copy-done, s32[16,32]{1,0:T(8,128)S(1)} %copy-done.1, f32[32,48,128]{2,1,0:T(8,128)S(1)} %collective-permute-done.got_on, f32[64,48,128]{2,1,0:T(8,128)S(1)} %get-tuple-element.15.ours, f32[8,48,128]{2,1,0:T(8,128)S(1)} %quarter.1.leaving), custom_call_target="tpu_custom_call" | custom-call | tf_op jit(solution)/shard_map/merge/pallas_call | solution.py:293
  23.5 4.3 %collective-permute-start.5 = (f32[32,48,128]{2,1,0:T(8,128)S(1)}, f32[32,48,128]{2,1,0:T(8,128)S(1)}, u32[]{:S(2)}, u32[]{:S(2)}) collective-permute-start(f32[32,48,128]{2,1,0:T(8,128)S(1)} %get-tuple-element.21), channel_id=1, source_target_pairs={{0,4},{4,0},{8,12},{12,8},{16,20},{20,16},{24,28},{28,24},{32,60},... | collective-permute-start | bytes 2359304 | tf_op jit(solution)/shard_map/ppermute | solution.py:36
  27.8 9.8 %collective-permute-start.4 = (f32[8,48,128]{2,1,0:T(8,128)S(1)}, f32[8,48,128]{2,1,0:T(8,128)S(1)}, u32[]{:S(2)}, u32[]{:S(2)}) collective-permute-start(f32[8,48,128]{2,1,0:T(8,128)S(1)} %quarter.1.leaving), channel_id=1, source_target_pairs={{32,67},{33,66},{34,65},{35,64},{64,35},{65,34},{66,33},{67,32},{9... | collective-permute-start | bytes 589832 | tf_op jit(solution)/shard_map/ppermute | solution.py:292
  37.7 9.5 %collective-permute-done.4.crossed = f32[8,48,128]{2,1,0:T(8,128)S(1)} collective-permute-done((f32[8,48,128]{2,1,0:T(8,128)S(1)}, f32[8,48,128]{2,1,0:T(8,128)S(1)}, u32[]{:S(2)}, u32[]{:S(2)}) %collective-permute-start.4) | collective-permute-done | bytes 196640 | tf_op jit(solution)/shard_map/ppermute | solution.py:292
  47.2 1.9 %collective-permute-start.6 = (f32[8,48,128]{2,1,0:T(8,128)S(1)}, f32[8,48,128]{2,1,0:T(8,128)S(1)}, u32[]{:S(2)}, u32[]{:S(2)}) collective-permute-start(f32[8,48,128]{2,1,0:T(8,128)S(1)} %collective-permute-done.4.crossed), channel_id=1, source_target_pairs={{0,4},{4,0},{8,12},{12,8},{16,20},{20,16},{24,28},{28,24},{32,60},... | collective-permute-start | bytes 589832 | tf_op jit(solution)/shard_map/ppermute | solution.py:36
  49.1 1.0 %shard_map.73.part = f32[32,48,128]{2,1,0:T(8,128)S(1)} custom-call(s32[16,32]{1,0:T(8,128)S(1)} %copy-done, s32[16,32]{1,0:T(8,128)S(1)} %copy-done.1, f32[32,48,128]{2,1,0:T(8,128)S(1)} %get-tuple-element.20.keep, f32[8,48,128]{2,1,0:T(8,128)S(1)} %collective-permute-done.4.crossed), custom_call_target="tpu_custom_call" | custom-call | flops 1048576 | bytes 4194304 | tf_op jit(solution)/shard_map/pallas_call | solution.py:305
  50.1 4.6 %collective-permute-done.6.passed = f32[8,48,128]{2,1,0:T(8,128)S(1)} collective-permute-done((f32[8,48,128]{2,1,0:T(8,128)S(1)}, f32[8,48,128]{2,1,0:T(8,128)S(1)}, u32[]{:S(2)}, u32[]{:S(2)}) %collective-permute-start.6) | collective-permute-done | bytes 196640 | tf_op jit(solution)/shard_map/ppermute | solution.py:36
  54.8 1.9 %shard_map.74 = f32[32,48,128]{2,1,0:T(8,128)} custom-call(s32[16,32]{1,0:T(8,128)S(1)} %copy-done, s32[16,32]{1,0:T(8,128)S(1)} %copy-done.1, f32[32,48,128]{2,1,0:T(8,128)S(1)} %shard_map.73.part, f32[32,48,128]{2,1,0:T(8,128)S(1)} %collective-permute-done.5.got, f32[8,48,128]{2,1,0:T(8,128)S(1)} %collective-permute-done.6.passed), custom_call_target="tpu_custom_call" | custom-call | flops 1048576 | bytes 4194304 | tf_op jit(solution)/shard_map/pallas_call | solution.py:305
  56.7 5.8 %all-to-all-start = ((f32[16,1,12288]{2,1,0:T(1,128)}), f32[16,1,12288]{2,1,0:T(1,128)S(1)}, u32[]{:S(2)}, u32[]{:S(2)}) async-start(f32[16,1,12288]{2,1,0:T(1,128)} %bitcast.4), calls=%async_computation | async-start | bytes 1572864 | tf_op jit(solution)/shard_map/all_to_all | solution.py:313
  62.4 0.1 divide_select_fusion
  62.5 0.1 broadcast_multiply_fusion
  62.6 0.1 mul.45.matrix
  62.7 0.2 reshape.34.precond
  62.9 0.2 spectral.1.part
  63.1 24.8 %all-to-all-done = f32[16,1,12288]{2,1,0:T(1,128)S(1)} async-done(((f32[16,1,12288]{2,1,0:T(1,128)}), f32[16,1,12288]{2,1,0:T(1,128)S(1)}, u32[]{:S(2)}, u32[]{:S(2)}) %all-to-all-start) | async-done | bytes 786464 | tf_op jit(solution)/shard_map/all_to_all | solution.py:313
  87.9 0.9 last.1
  (13 shorter events, 0.1 us)
Async XLA Ops:
  0.0 22.0 %copy-start = (s32[16,32]{1,0:T(8,128)S(1)}, s32[16,32]{1,0:T(8,128)}, u32[]{:S(2)}) copy-start(s32[16,32]{1,0:T(8,128)} %lower.5) | copy-start | bytes 6148
  0.0 22.0 %copy-start.1 = (s32[16,32]{1,0:T(8,128)S(1)}, s32[16,32]{1,0:T(8,128)}, u32[]{:S(2)}) copy-start(s32[16,32]{1,0:T(8,128)} %upper.5) | copy-start | bytes 6148
  3.7 18.3 %collective-permute-start = (f32[32,48,128]{2,1,0:T(8,128)S(1)}, f32[32,48,128]{2,1,0:T(8,128)S(1)}, u32[]{:S(2)}, u32[]{:S(2)}) collective-permute-start(f32[32,48,128]{2,1,0:T(8,128)S(1)} %get-tuple-element.14), channel_id=1, source_target_pairs={{0,32},{32,0},{1,33},{33,1},{2,34},{34,2},{3,35},{35,3},{4,36},{36... | collective-permute-start | bytes 2359304 | tf_op jit(solution)/shard_map/ppermute | solution.py:283
  5.7 9.8 %collective-permute-start.1 = (f32[8,48,128]{2,1,0:T(8,128)S(1)}, f32[8,48,128]{2,1,0:T(8,128)S(1)}, u32[]{:S(2)}, u32[]{:S(2)}) collective-permute-start(f32[8,48,128]{2,1,0:T(8,128)S(1)} %get-tuple-element.16), channel_id=1, source_target_pairs={{0,1},{1,0},{2,3},{3,2},{4,5},{5,4},{6,7},{7,6},{8,9},{9,8},{10,11... | collective-permute-start | bytes 589832 | tf_op jit(solution)/shard_map/ppermute | solution.py:40
  10.0 7.6 %collective-permute-start.2 = (f32[8,48,128]{2,1,0:T(8,128)S(1)}, f32[8,48,128]{2,1,0:T(8,128)S(1)}, u32[]{:S(2)}, u32[]{:S(2)}) collective-permute-start(f32[8,48,128]{2,1,0:T(8,128)S(1)} %get-tuple-element.17), channel_id=1, source_target_pairs={{0,4},{4,0},{8,12},{12,8},{16,20},{20,16},{24,28},{28,24},{32,60},... | collective-permute-start | bytes 589832 | tf_op jit(solution)/shard_map/ppermute | solution.py:36
  13.5 8.5 %collective-permute-start.3 = (f32[8,48,128]{2,1,0:T(8,128)S(1)}, f32[8,48,128]{2,1,0:T(8,128)S(1)}, u32[]{:S(2)}, u32[]{:S(2)}) collective-permute-start(f32[8,48,128]{2,1,0:T(8,128)S(1)} %get-tuple-element.18), channel_id=1, source_target_pairs={{0,5},{1,4},{4,1},{5,0},{8,13},{9,12},{12,9},{13,8},{16,21},{17,20... | collective-permute-start | bytes 589832 | tf_op jit(solution)/shard_map/ppermute | solution.py:50
  23.5 31.3 %collective-permute-start.5 = (f32[32,48,128]{2,1,0:T(8,128)S(1)}, f32[32,48,128]{2,1,0:T(8,128)S(1)}, u32[]{:S(2)}, u32[]{:S(2)}) collective-permute-start(f32[32,48,128]{2,1,0:T(8,128)S(1)} %get-tuple-element.21), channel_id=1, source_target_pairs={{0,4},{4,0},{8,12},{12,8},{16,20},{20,16},{24,28},{28,24},{32,60},... | collective-permute-start | bytes 2359304 | tf_op jit(solution)/shard_map/ppermute | solution.py:36
  27.8 19.4 %collective-permute-start.4 = (f32[8,48,128]{2,1,0:T(8,128)S(1)}, f32[8,48,128]{2,1,0:T(8,128)S(1)}, u32[]{:S(2)}, u32[]{:S(2)}) collective-permute-start(f32[8,48,128]{2,1,0:T(8,128)S(1)} %quarter.1.leaving), channel_id=1, source_target_pairs={{32,67},{33,66},{34,65},{35,64},{64,35},{65,34},{66,33},{67,32},{9... | collective-permute-start | bytes 589832 | tf_op jit(solution)/shard_map/ppermute | solution.py:292
  47.2 7.6 %collective-permute-start.6 = (f32[8,48,128]{2,1,0:T(8,128)S(1)}, f32[8,48,128]{2,1,0:T(8,128)S(1)}, u32[]{:S(2)}, u32[]{:S(2)}) collective-permute-start(f32[8,48,128]{2,1,0:T(8,128)S(1)} %collective-permute-done.4.crossed), channel_id=1, source_target_pairs={{0,4},{4,0},{8,12},{12,8},{16,20},{20,16},{24,28},{28,24},{32,60},... | collective-permute-start | bytes 589832 | tf_op jit(solution)/shard_map/ppermute | solution.py:36
  50.1 12.6 %copy-start.3 = (bf16[2,36864]{1,0:T(2,128)(2,1)S(1)}, bf16[2,36864]{1,0:T(2,128)(2,1)}, u32[]{:S(2)}) copy-start(bf16[2,36864]{1,0:T(2,128)(2,1)} %param.11) | copy-start | bytes 442372
  50.1 12.8 %copy-start.2 = (f32[2,192]{1,0:T(2,128)S(1)}, f32[2,192]{1,0:T(2,128)}, u32[]{:S(2)}) copy-start(f32[2,192]{1,0:T(2,128)} %rates.1) | copy-start | bytes 4612
  56.7 31.2 %all-to-all-start = ((f32[16,1,12288]{2,1,0:T(1,128)}), f32[16,1,12288]{2,1,0:T(1,128)S(1)}, u32[]{:S(2)}, u32[]{:S(2)}) async-start(f32[16,1,12288]{2,1,0:T(1,128)} %bitcast.4), calls=%async_computation | async-start | bytes 1572864 | tf_op jit(solution)/shard_map/all_to_all | solution.py:313

commit v4 on v3

--- a/solution.py
+++ b/solution.py
@@ -64,7 +64,7 @@
 
 
 def row_of(block):
-    return (((block >> 1) & 3) << 3) + ((block >> 4) << 1) + (block & 1)
+    return ((block >> 4) << 3) + (block & 7)
 
 
 def parity_of(block):
@@ -140,7 +140,7 @@
             )
             planes = jnp.concatenate([main, tail], axis=0)
             if k == 0:
-                target = lax.axis_index("zq") * 16 + lax.axis_index("zp") * 8 + lax.axis_index("yh") * 2 + b
+                target = lax.axis_index("yh") * 8 + lax.axis_index("zq") * 4 + lax.axis_index("zp") * 2 + b
             else:
                 c = columns[b, k - 1]
                 slot = c - off_base
@@ -310,7 +310,7 @@
             compiler_params=pltpu.CompilerParams(vmem_limit_bytes=16 * 2**20),
             cost_estimate=pl.CostEstimate(flops=2**20, bytes_accessed=2**22, transcendentals=0),
         )(lower_list, upper_list, merged, *arrays)
-    shared = lax.all_to_all(merged.reshape(16, -1), ("zq", "zp", "yh"), 0, 0, tiled=True)
+    shared = lax.all_to_all(merged.reshape(16, -1), ("yh", "zq", "zp"), 0, 0, tiled=True)
 
     half = jnp.pad(spectral_matrix(INST).T, ((0, 1), (0, 1)))
     matrix = jnp.kron(jnp.eye(ADJ, dtype=jnp.float32), half)

time: 89.8 us -> 87.9 us (0.979)
  waiting for transfers between devices: 45.6 us -> 44.4 us
    all_to_all x1, waiting for transfers between devices: 24.8 us -> 23.6 us  [shards(): lax.all_to_all(merged.reshape(16, -1), ('yh', 'zq', 'zp'), 0, 0, tiled=True)]
  transfers between devices with their start and end apart: 8 -> 8, of which waited for: 6 -> 6; matrix products, arithmetic and copies ran while one was open for 0% -> 1% of each run, Pallas kernels for 1% -> 1%
where the time goes in v4:
time: 87.9 us; the launch traced here: 87.5 us
  waiting for transfers between devices  44.4 us (51%)
  starting transfers between devices  33.4 us (38%)
  Pallas kernels  9.05 us (10%)
    all_to_all x1, waiting for transfers between devices, shards(): lax.all_to_all(merged.reshape(16, -1), ('yh', 'zq', 'zp'), 0, 0, tiled=True)  23.6 us
    ppermute x1, starting transfers between devices, shards(): lax.ppermute(leaving, ('x', 'zh', 'core', 'zq', 'zp'), off_chip_pairs())  9.81 us
    ppermute x3, starting transfers between devices, to_mate(): return lax.ppermute(value, ('core', 'yh', 'yp'), pairs)  9.72 us
    ppermute x1, waiting for transfers between devices, shards(): lax.ppermute(leaving, ('x', 'zh', 'core', 'zq', 'zp'), off_chip_pairs())  9.54 us
    ppermute x3, waiting for transfers between devices, to_mate(): return lax.ppermute(value, ('core', 'yh', 'yp'), pairs)  6.67 us
    all_to_all x1, starting transfers between devices, shards(): lax.all_to_all(merged.reshape(16, -1), ('yh', 'zq', 'zp'), 0, 0, tiled=True)  5.76 us
    ppermute x1, waiting for transfers between devices, to_mates_side(): return lax.ppermute(value, ('core', 'yh', 'yp', 'zp'), pairs)  4.43 us
    ppermute x1, starting transfers between devices, to_side(): return lax.ppermute(value, 'zp', [(0, 1), (1, 0)])  4.28 us
  transfers between devices with their start and end apart: 8, of which 6 were waited for; matrix products, arithmetic and copies ran while one was open for 1% of the time, Pallas kernels for 1%

profile of v4, /device:TPU:6, one launch (start us, length us, event | category | flops | bytes accessed | tf_op | source)
XLA Modules:
  0.0 87.5 jit_solution(8011122163283350745)
XLA Ops:
  0.0 3.7 %terms.1 = (f32[64,48,128]{2,1,0:T(8,128)S(1)}, f32[8,48,128]{2,1,0:T(8,128)S(1)}, f32[8,48,128]{2,1,0:T(8,128)S(1)}, f32[8,48,128]{2,1,0:T(8,128)S(1)}, f32[8,4...) custom-call(s32[2,16]{1,0:T(2,128)} %columns_in.1, bf16[30,2,192]{2,1,0:T(2,128)(2,1)} %bitcast.11, ...), custom_call_target="tpu_custom_call" | custom-call | tf_op jit(solution)/shard_map/terms/pallas_call | solution.py:262
  3.7 1.9 %collective-permute-start = (f32[32,48,128]{2,1,0:T(8,128)S(1)}, f32[32,48,128]{2,1,0:T(8,128)S(1)}, u32[]{:S(2)}, u32[]{:S(2)}) collective-permute-start(f32[32,48,128]{2,1,0:T(8,128)S(1)} %get-tuple-element.14), channel_id=1, source_target_pairs={{0,32},{32,0},{1,33},{33,1},{2,34},{34,2},{3,35},{35,3},{4,36},{36... | collective-permute-start | bytes 2359304 | tf_op jit(solution)/shard_map/ppermute | solution.py:283
  5.6 4.3 %collective-permute-start.1 = (f32[8,48,128]{2,1,0:T(8,128)S(1)}, f32[8,48,128]{2,1,0:T(8,128)S(1)}, u32[]{:S(2)}, u32[]{:S(2)}) collective-permute-start(f32[8,48,128]{2,1,0:T(8,128)S(1)} %get-tuple-element.16), channel_id=1, source_target_pairs={{0,1},{1,0},{2,3},{3,2},{4,5},{5,4},{6,7},{7,6},{8,9},{9,8},{10,11... | collective-permute-start | bytes 589832 | tf_op jit(solution)/shard_map/ppermute | solution.py:40
  9.9 3.5 %collective-permute-start.2 = (f32[8,48,128]{2,1,0:T(8,128)S(1)}, f32[8,48,128]{2,1,0:T(8,128)S(1)}, u32[]{:S(2)}, u32[]{:S(2)}) collective-permute-start(f32[8,48,128]{2,1,0:T(8,128)S(1)} %get-tuple-element.17), channel_id=1, source_target_pairs={{0,4},{4,0},{8,12},{12,8},{16,20},{20,16},{24,28},{28,24},{32,60},... | collective-permute-start | bytes 589832 | tf_op jit(solution)/shard_map/ppermute | solution.py:36
  13.4 1.9 %collective-permute-start.3 = (f32[8,48,128]{2,1,0:T(8,128)S(1)}, f32[8,48,128]{2,1,0:T(8,128)S(1)}, u32[]{:S(2)}, u32[]{:S(2)}) collective-permute-start(f32[8,48,128]{2,1,0:T(8,128)S(1)} %get-tuple-element.18), channel_id=1, source_target_pairs={{0,5},{1,4},{4,1},{5,0},{8,13},{9,12},{12,9},{13,8},{16,21},{17,20... | collective-permute-start | bytes 589832 | tf_op jit(solution)/shard_map/ppermute | solution.py:50
  15.4 0.1 collective-permute-done.1.side
  15.5 2.0 %collective-permute-done.2.mate = f32[8,48,128]{2,1,0:T(8,128)S(1)} collective-permute-done((f32[8,48,128]{2,1,0:T(8,128)S(1)}, f32[8,48,128]{2,1,0:T(8,128)S(1)}, u32[]{:S(2)}, u32[]{:S(2)}) %collective-permute-start.2) | collective-permute-done | bytes 196640 | tf_op jit(solution)/shard_map/ppermute | solution.py:36
  17.5 4.4 %collective-permute-done.3.cross = f32[8,48,128]{2,1,0:T(8,128)S(1)} collective-permute-done((f32[8,48,128]{2,1,0:T(8,128)S(1)}, f32[8,48,128]{2,1,0:T(8,128)S(1)}, u32[]{:S(2)}, u32[]{:S(2)}) %collective-permute-start.3) | collective-permute-done | bytes 196640 | tf_op jit(solution)/shard_map/ppermute | solution.py:50
  22.0 1.4 %merge.1 = (f32[32,48,128]{2,1,0:T(8,128)S(1)}, f32[32,48,128]{2,1,0:T(8,128)S(1)}) custom-call(s32[16,32]{1,0:T(8,128)S(1)} %copy-done, s32[16,32]{1,0:T(8,128)S(1)} %copy-done.1, f32[32,48,128]{2,1,0:T(8,128)S(1)} %collective-permute-done.got_on, f32[64,48,128]{2,1,0:T(8,128)S(1)} %get-tuple-element.15.ours, f32[8,48,128]{2,1,0:T(8,128)S(1)} %quarter.1.leaving), custom_call_target="tpu_custom_call" | custom-call | tf_op jit(solution)/shard_map/merge/pallas_call | solution.py:293
  23.4 4.3 %collective-permute-start.5 = (f32[32,48,128]{2,1,0:T(8,128)S(1)}, f32[32,48,128]{2,1,0:T(8,128)S(1)}, u32[]{:S(2)}, u32[]{:S(2)}) collective-permute-start(f32[32,48,128]{2,1,0:T(8,128)S(1)} %get-tuple-element.21), channel_id=1, source_target_pairs={{0,4},{4,0},{8,12},{12,8},{16,20},{20,16},{24,28},{28,24},{32,60},... | collective-permute-start | bytes 2359304 | tf_op jit(solution)/shard_map/ppermute | solution.py:36
  27.8 9.8 %collective-permute-start.4 = (f32[8,48,128]{2,1,0:T(8,128)S(1)}, f32[8,48,128]{2,1,0:T(8,128)S(1)}, u32[]{:S(2)}, u32[]{:S(2)}) collective-permute-start(f32[8,48,128]{2,1,0:T(8,128)S(1)} %quarter.1.leaving), channel_id=1, source_target_pairs={{32,67},{33,66},{34,65},{35,64},{64,35},{65,34},{66,33},{67,32},{9... | collective-permute-start | bytes 589832 | tf_op jit(solution)/shard_map/ppermute | solution.py:292
  37.6 9.5 %collective-permute-done.4.crossed = f32[8,48,128]{2,1,0:T(8,128)S(1)} collective-permute-done((f32[8,48,128]{2,1,0:T(8,128)S(1)}, f32[8,48,128]{2,1,0:T(8,128)S(1)}, u32[]{:S(2)}, u32[]{:S(2)}) %collective-permute-start.4) | collective-permute-done | bytes 196640 | tf_op jit(solution)/shard_map/ppermute | solution.py:292
  47.2 1.9 %collective-permute-start.6 = (f32[8,48,128]{2,1,0:T(8,128)S(1)}, f32[8,48,128]{2,1,0:T(8,128)S(1)}, u32[]{:S(2)}, u32[]{:S(2)}) collective-permute-start(f32[8,48,128]{2,1,0:T(8,128)S(1)} %collective-permute-done.4.crossed), channel_id=1, source_target_pairs={{0,4},{4,0},{8,12},{12,8},{16,20},{20,16},{24,28},{28,24},{32,60},... | collective-permute-start | bytes 589832 | tf_op jit(solution)/shard_map/ppermute | solution.py:36
  49.1 0.9 %shard_map.73.part = f32[32,48,128]{2,1,0:T(8,128)S(1)} custom-call(s32[16,32]{1,0:T(8,128)S(1)} %copy-done, s32[16,32]{1,0:T(8,128)S(1)} %copy-done.1, f32[32,48,128]{2,1,0:T(8,128)S(1)} %get-tuple-element.20.keep, f32[8,48,128]{2,1,0:T(8,128)S(1)} %collective-permute-done.4.crossed), custom_call_target="tpu_custom_call" | custom-call | flops 1048576 | bytes 4194304 | tf_op jit(solution)/shard_map/pallas_call | solution.py:305
  50.0 4.7 %collective-permute-done.6.passed = f32[8,48,128]{2,1,0:T(8,128)S(1)} collective-permute-done((f32[8,48,128]{2,1,0:T(8,128)S(1)}, f32[8,48,128]{2,1,0:T(8,128)S(1)}, u32[]{:S(2)}, u32[]{:S(2)}) %collective-permute-start.6) | collective-permute-done | bytes 196640 | tf_op jit(solution)/shard_map/ppermute | solution.py:36
  54.7 1.9 %shard_map.74 = f32[32,48,128]{2,1,0:T(8,128)} custom-call(s32[16,32]{1,0:T(8,128)S(1)} %copy-done, s32[16,32]{1,0:T(8,128)S(1)} %copy-done.1, f32[32,48,128]{2,1,0:T(8,128)S(1)} %shard_map.73.part, f32[32,48,128]{2,1,0:T(8,128)S(1)} %collective-permute-done.5.got, f32[8,48,128]{2,1,0:T(8,128)S(1)} %collective-permute-done.6.passed), custom_call_target="tpu_custom_call" | custom-call | flops 1048576 | bytes 4194304 | tf_op jit(solution)/shard_map/pallas_call | solution.py:305
  56.6 5.8 %all-to-all-start = ((f32[16,1,12288]{2,1,0:T(1,128)}), f32[16,1,12288]{2,1,0:T(1,128)S(1)}, u32[]{:S(2)}, u32[]{:S(2)}) async-start(f32[16,1,12288]{2,1,0:T(1,128)} %bitcast.4), calls=%async_computation | async-start | bytes 1572864 | tf_op jit(solution)/shard_map/all_to_all | solution.py:313
  62.4 0.1 divide_select_fusion
  62.5 0.1 broadcast_multiply_fusion
  62.5 0.1 mul.45.matrix
  62.6 0.2 reshape.34.precond
  62.8 0.2 spectral.1.part
  63.0 23.6 %all-to-all-done = f32[16,1,12288]{2,1,0:T(1,128)S(1)} async-done(((f32[16,1,12288]{2,1,0:T(1,128)}), f32[16,1,12288]{2,1,0:T(1,128)S(1)}, u32[]{:S(2)}, u32[]{:S(2)}) %all-to-all-start) | async-done | bytes 786464 | tf_op jit(solution)/shard_map/all_to_all | solution.py:313
  86.7 0.9 last.1
  (13 shorter events, 0.1 us)
Async XLA Ops:
  0.0 22.0 %copy-start = (s32[16,32]{1,0:T(8,128)S(1)}, s32[16,32]{1,0:T(8,128)}, u32[]{:S(2)}) copy-start(s32[16,32]{1,0:T(8,128)} %lower.5) | copy-start | bytes 6148
  0.0 22.0 %copy-start.1 = (s32[16,32]{1,0:T(8,128)S(1)}, s32[16,32]{1,0:T(8,128)}, u32[]{:S(2)}) copy-start(s32[16,32]{1,0:T(8,128)} %upper.5) | copy-start | bytes 6148
  3.7 18.3 %collective-permute-start = (f32[32,48,128]{2,1,0:T(8,128)S(1)}, f32[32,48,128]{2,1,0:T(8,128)S(1)}, u32[]{:S(2)}, u32[]{:S(2)}) collective-permute-start(f32[32,48,128]{2,1,0:T(8,128)S(1)} %get-tuple-element.14), channel_id=1, source_target_pairs={{0,32},{32,0},{1,33},{33,1},{2,34},{34,2},{3,35},{35,3},{4,36},{36... | collective-permute-start | bytes 2359304 | tf_op jit(solution)/shard_map/ppermute | solution.py:283
  5.6 9.8 %collective-permute-start.1 = (f32[8,48,128]{2,1,0:T(8,128)S(1)}, f32[8,48,128]{2,1,0:T(8,128)S(1)}, u32[]{:S(2)}, u32[]{:S(2)}) collective-permute-start(f32[8,48,128]{2,1,0:T(8,128)S(1)} %get-tuple-element.16), channel_id=1, source_target_pairs={{0,1},{1,0},{2,3},{3,2},{4,5},{5,4},{6,7},{7,6},{8,9},{9,8},{10,11... | collective-permute-start | bytes 589832 | tf_op jit(solution)/shard_map/ppermute | solution.py:40
  9.9 7.6 %collective-permute-start.2 = (f32[8,48,128]{2,1,0:T(8,128)S(1)}, f32[8,48,128]{2,1,0:T(8,128)S(1)}, u32[]{:S(2)}, u32[]{:S(2)}) collective-permute-start(f32[8,48,128]{2,1,0:T(8,128)S(1)} %get-tuple-element.17), channel_id=1, source_target_pairs={{0,4},{4,0},{8,12},{12,8},{16,20},{20,16},{24,28},{28,24},{32,60},... | collective-permute-start | bytes 589832 | tf_op jit(solution)/shard_map/ppermute | solution.py:36
  13.4 8.5 %collective-permute-start.3 = (f32[8,48,128]{2,1,0:T(8,128)S(1)}, f32[8,48,128]{2,1,0:T(8,128)S(1)}, u32[]{:S(2)}, u32[]{:S(2)}) collective-permute-start(f32[8,48,128]{2,1,0:T(8,128)S(1)} %get-tuple-element.18), channel_id=1, source_target_pairs={{0,5},{1,4},{4,1},{5,0},{8,13},{9,12},{12,9},{13,8},{16,21},{17,20... | collective-permute-start | bytes 589832 | tf_op jit(solution)/shard_map/ppermute | solution.py:50
  23.4 31.3 %collective-permute-start.5 = (f32[32,48,128]{2,1,0:T(8,128)S(1)}, f32[32,48,128]{2,1,0:T(8,128)S(1)}, u32[]{:S(2)}, u32[]{:S(2)}) collective-permute-start(f32[32,48,128]{2,1,0:T(8,128)S(1)} %get-tuple-element.21), channel_id=1, source_target_pairs={{0,4},{4,0},{8,12},{12,8},{16,20},{20,16},{24,28},{28,24},{32,60},... | collective-permute-start | bytes 2359304 | tf_op jit(solution)/shard_map/ppermute | solution.py:36
  27.8 19.4 %collective-permute-start.4 = (f32[8,48,128]{2,1,0:T(8,128)S(1)}, f32[8,48,128]{2,1,0:T(8,128)S(1)}, u32[]{:S(2)}, u32[]{:S(2)}) collective-permute-start(f32[8,48,128]{2,1,0:T(8,128)S(1)} %quarter.1.leaving), channel_id=1, source_target_pairs={{32,67},{33,66},{34,65},{35,64},{64,35},{65,34},{66,33},{67,32},{9... | collective-permute-start | bytes 589832 | tf_op jit(solution)/shard_map/ppermute | solution.py:292
  47.2 7.6 %collective-permute-start.6 = (f32[8,48,128]{2,1,0:T(8,128)S(1)}, f32[8,48,128]{2,1,0:T(8,128)S(1)}, u32[]{:S(2)}, u32[]{:S(2)}) collective-permute-start(f32[8,48,128]{2,1,0:T(8,128)S(1)} %collective-permute-done.4.crossed), channel_id=1, source_target_pairs={{0,4},{4,0},{8,12},{12,8},{16,20},{20,16},{24,28},{28,24},{32,60},... | collective-permute-start | bytes 589832 | tf_op jit(solution)/shard_map/ppermute | solution.py:36
  50.0 12.6 %copy-start.3 = (bf16[2,36864]{1,0:T(2,128)(2,1)S(1)}, bf16[2,36864]{1,0:T(2,128)(2,1)}, u32[]{:S(2)}) copy-start(bf16[2,36864]{1,0:T(2,128)(2,1)} %param.11) | copy-start | bytes 442372
  50.0 12.8 %copy-start.2 = (f32[2,192]{1,0:T(2,128)S(1)}, f32[2,192]{1,0:T(2,128)}, u32[]{:S(2)}) copy-start(f32[2,192]{1,0:T(2,128)} %rates.1) | copy-start | bytes 4612
  56.6 30.1 %all-to-all-start = ((f32[16,1,12288]{2,1,0:T(1,128)}), f32[16,1,12288]{2,1,0:T(1,128)S(1)}, u32[]{:S(2)}, u32[]{:S(2)}) async-start(f32[16,1,12288]{2,1,0:T(1,128)} %bitcast.4), calls=%async_computation | async-start | bytes 1572864 | tf_op jit(solution)/shard_map/all_to_all | solution.py:313
